TPU v7x, 512 devices: a whole 4x4x16 slice. The times are simulated.
512 devices in a mesh: gx: 32 (over z, x_lo), gy: 16 (over x_hi, y, core).
Axes of the slice: x: 4 (x_hi: 2, x_lo: 2; x = x_hi * 2 + x_lo), y: 4, z: 16, core: 2. Of those that a mesh axis runs over, the one named last changes fastest.
Arguments:
- disp: float32 [2, 256, 16384], P(None, 'gx', 'gy'), may hold values from -0.2 to 0.2
- vel: float32 [2, 256, 16384], P(None, 'gx', 'gy'), may hold values from -1 to 1
- bonds: int32 [4, 256, 16384], P(None, 'gx', 'gy'), may hold values from 0 to 127, as said below
Outputs:
- new_disp: float32 [2, 256, 16384], P(None, 'gx', 'gy')
- new_vel: float32 [2, 256, 16384], P(None, 'gx', 'gy')
Inputs may be any that keep to these rules, and one draw needn't show every extreme that they name: `bonds`: bit j of word 0 is bit j of the table's word 0 (j < 3), bits 0 to 6 of words 1 to 3 likewise; word 0 is below 8 and no higher bits are set.
All inputs are finite; a program needn't handle non-finite values.
Results may differ from a plain program's by a relative error of at most 0.00002.
Values sent between devices are 32-bit elements; how exact they have to be, the bound alone decides.
No kernel may reach another device: no remote copies, remote signals or barrier semaphores. Data moves between devices by JAX's collectives and lax.ppermute only.
A program may use at most 64 MiB of HBM per device.

v0:
```python
import math

import jax
import jax.numpy as jnp
from jax import lax
from jax.sharding import PartitionSpec as P

STEPS = 2


STIFFNESS = 40.0
DAMPING = 1.0
TIME_STEP = 0.05
SOFTENING = 0.0625
BOND_TABLE = [(0, c, 0, c - 1) for c in (1, 2, 3)] + [
    (r, c, r, c + 3) for r in (1, 2, 3) for c in (-3, -2, -1, 0, 1, 2, 3)
]
PACK_SHIFT = (0, 3, 10, 17)


def extended(block, sides, width):
    for axis, dim in sides:
        count = lax.axis_size(axis)
        forward = [(i, i + 1) for i in range(count - 1)]
        forward.append((count - 1, 0))
        backward = [(target, source) for source, target in forward]
        low = lax.ppermute(
            lax.slice_in_dim(block, block.shape[dim] - width, None, axis=dim), axis, forward
        )
        high = lax.ppermute(lax.slice_in_dim(block, 0, width, axis=dim), axis, backward)
        block = jnp.concatenate([low, block, high], axis=dim)
    return block


def passed_along(array, axis, by):
    devices = lax.axis_size(axis)
    return lax.ppermute(array, axis, [(i, (i + by) % devices) for i in range(devices)])


def bond_force(near_state, far_state, row_off, col_off, intact):
    length = math.sqrt(row_off * row_off + col_off * col_off)
    rest = math.sqrt(length * length + SOFTENING)
    along_x = row_off + far_state[0] - near_state[0]
    along_y = col_off + far_state[1] - near_state[1]
    stretched = jnp.sqrt(along_x * along_x + along_y * along_y + SOFTENING)
    strain = (stretched - rest) / length
    closing = (
        along_x * (far_state[2] - near_state[2]) + along_y * (far_state[3] - near_state[3])
    ) / (stretched * length)
    tension = intact * (STIFFNESS * strain + DAMPING * closing) / length
    return (tension * along_x / stretched, tension * along_y / stretched)


def intact_bits(word_array, bit):
    return jnp.bitwise_and(jnp.right_shift(word_array, bit), 1).astype(jnp.float32)


def twice_force(state, bonds, mask_box, row_count, col_count):
    padded_state = extended(state, (("gx", 1), ("gy", 2)), 3)
    own_state = padded_state[:, 3 : 3 + row_count, 3 : 3 + col_count]
    force_x = jnp.zeros((row_count, col_count), jnp.float32)
    force_y = jnp.zeros((row_count, col_count), jnp.float32)
    for row_off, col_off, word, bit in BOND_TABLE:
        far_state = padded_state[
            :, 3 + row_off : 3 + row_off + row_count, 3 + col_off : 3 + col_off + col_count
        ]
        pull_x, pull_y = bond_force(
            own_state, far_state, row_off, col_off, intact_bits(bonds[word], bit)
        )
        near_state = padded_state[
            :, 3 - row_off : 3 - row_off + row_count, 3 - col_off : 3 - col_off + col_count
        ]
        near_words = mask_box[
            3 - row_off : 3 - row_off + row_count, 3 - col_off : 3 - col_off + col_count
        ]
        push_x, push_y = bond_force(
            near_state, own_state, row_off, col_off, intact_bits(near_words, PACK_SHIFT[word] + bit)
        )
        force_x = force_x + pull_x - push_x
        force_y = force_y + pull_y - push_y
    return jnp.stack([force_x, force_y])


def per_device(disp, vel, bonds):
    row_count = disp.shape[1]
    col_count = disp.shape[2]
    packed = bonds[0] + bonds[1] * 8 + bonds[2] * 1024 + bonds[3] * 131072
    earlier = passed_along(packed[row_count - 3 :, :], "gx", 1)
    mask_box = extended(jnp.concatenate([earlier, packed], 0), (("gy", 1),), 3)

    def forces(state):
        return twice_force(state, bonds, mask_box, row_count, col_count)

    acceleration = forces(jnp.concatenate([disp, vel], 0))
    for step in range(STEPS):
        half_vel = vel + 0.5 * TIME_STEP * acceleration
        disp = disp + TIME_STEP * half_vel
        acceleration = forces(jnp.concatenate([disp, half_vel], 0))
        vel = half_vel + 0.5 * TIME_STEP * acceleration
    return (disp, vel)


def solution(mesh):
    in_specs = (P(None, "gx", "gy"), P(None, "gx", "gy"), P(None, "gx", "gy"))
    out_specs = (P(None, "gx", "gy"), P(None, "gx", "gy"))
    return jax.shard_map(
        per_device, mesh=mesh, in_specs=in_specs, out_specs=out_specs, check_vma=False
    )
```

profile of v0, /device:TPU:25, one launch (start us, length us, event | category | flops | bytes accessed | tf_op | source)
XLA Modules:
  0.0 102.7 jit_solution(7546503874815211096)
XLA Ops:
  0.6 0.9 multiply_add_fusion.2
  1.5 0.0 copy-start.2
  1.5 3.3 %collective-permute-start.3 = (s32[3,1024]{1,0:T(4,128)S(1)}, s32[3,1024]{1,0:T(4,128)S(1)}, u32[]{:S(2)}, u32[]{:S(2)}) collective-permute-start(s32[3,1024]{1,0:T(4,128)S(1)} %slice_bitcast_fusion), channel_id=1, source_target_pairs={{0,16},{16,32},{32,48},{48,64},{64,80},{80,96},{96,112},{112,128},... | collective-permute-start | bytes 36872 | tf_op jit(solution)/shard_map/ppermute | solution.py:37
  4.8 0.0 copy-start
  4.9 11.0 %collective-permute-start.1 = (f32[4,3,1024]{2,1,0:T(4,128)S(1)}, f32[4,3,1024]{2,1,0:T(4,128)S(1)}, u32[]{:S(2)}, u32[]{:S(2)}) collective-permute-start(f32[4,3,1024]{2,1,0:T(4,128)S(1)} %get-tuple-element.109), channel_id=1, source_target_pairs={{16,0},{32,16},{48,32},{64,48},{80,64},{96,80},{112,96},{128,112},... | collective-permute-start | bytes 147464 | tf_op jit(solution)/shard_map/ppermute | solution.py:30
  15.9 0.1 pad_add_fusion.2
  16.0 2.9 %collective-permute-start.6 = (s32[11,3]{1,0:T(8,128)S(1)}, s32[11,3]{1,0:T(8,128)S(1)}, u32[]{:S(2)}, u32[]{:S(2)}) collective-permute-start(s32[11,3]{1,0:T(8,128)S(1)} %get-tuple-element.113), channel_id=1, source_target_pairs={{1,0},{2,1},{3,2},{4,3},{5,4},{6,5},{7,6},{8,7},{9,8},{10,9},{11,1... | collective-permute-start | bytes 404 | tf_op jit(solution)/shard_map/ppermute | solution.py:30
  18.8 6.3 %collective-permute-start.4 = (s32[11,3]{1,0:T(8,128)S(1)}, s32[11,3]{1,0:T(8,128)S(1)}, u32[]{:S(2)}, u32[]{:S(2)}) collective-permute-start(s32[11,3]{1,0:T(8,128)S(1)} %get-tuple-element.114), channel_id=1, source_target_pairs={{0,1},{1,2},{2,3},{3,4},{4,5},{5,6},{6,7},{7,8},{8,9},{9,10},{10,1... | collective-permute-start | bytes 404 | tf_op jit(solution)/shard_map/ppermute | solution.py:27
  25.2 1.9 %collective-permute-start = (f32[4,3,1024]{2,1,0:T(4,128)S(1)}, f32[4,3,1024]{2,1,0:T(4,128)S(1)}, u32[]{:S(2)}, u32[]{:S(2)}) collective-permute-start(f32[4,3,1024]{2,1,0:T(4,128)S(1)} %get-tuple-element.110), channel_id=1, source_target_pairs={{0,16},{16,32},{32,48},{48,64},{64,80},{80,96},{96,112},{112,128},... | collective-permute-start | bytes 147464 | tf_op jit(solution)/shard_map/ppermute | solution.py:27
  27.1 0.0 collective-permute-done.6
  27.1 0.0 collective-permute-done.4
  27.1 0.1 pad_add_fusion
  27.2 5.1 %collective-permute-done = f32[4,3,1024]{2,1,0:T(4,128)S(1)} collective-permute-done((f32[4,3,1024]{2,1,0:T(4,128)S(1)}, f32[4,3,1024]{2,1,0:T(4,128)S(1)}, u32[]{:S(2)}, u32[]{:S(2)}) %collective-permute-start) | collective-permute-done | bytes 49184 | tf_op jit(solution)/shard_map/ppermute | solution.py:27
  32.3 0.1 pad_maximum_fusion.17
  32.4 3.1 %collective-permute-start.5 = (f32[4,14,3]{2,1,0:T(8,128)S(1)}, f32[4,14,3]{2,1,0:T(8,128)S(1)}, u32[]{:S(2)}, u32[]{:S(2)}) collective-permute-start(f32[4,14,3]{2,1,0:T(8,128)S(1)} %get-tuple-element.99), channel_id=1, source_target_pairs={{0,1},{1,2},{2,3},{3,4},{4,5},{5,6},{6,7},{7,8},{8,9},{9,10},{10,1... | collective-permute-start | bytes 2024 | tf_op jit(solution)/shard_map/ppermute | solution.py:27
  35.5 1.9 %collective-permute-start.2 = (f32[4,14,3]{2,1,0:T(8,128)S(1)}, f32[4,14,3]{2,1,0:T(8,128)S(1)}, u32[]{:S(2)}, u32[]{:S(2)}) collective-permute-start(f32[4,14,3]{2,1,0:T(8,128)S(1)} %get-tuple-element.100), channel_id=1, source_target_pairs={{1,0},{2,1},{3,2},{4,3},{5,4},{6,5},{7,6},{8,7},{9,8},{10,9},{11,1... | collective-permute-start | bytes 2024 | tf_op jit(solution)/shard_map/ppermute | solution.py:30
  37.4 0.1 fusion.1800
  37.5 0.1 fusion.1799
  37.5 0.1 fusion.1797
  37.6 0.1 fusion.1798
  37.7 6.6 %collective-permute-done.2 = f32[4,14,3]{2,1,0:T(8,128)S(1)} collective-permute-done((f32[4,14,3]{2,1,0:T(8,128)S(1)}, f32[4,14,3]{2,1,0:T(8,128)S(1)}, u32[]{:S(2)}, u32[]{:S(2)}) %collective-permute-start.2) | collective-permute-done | bytes 704 | tf_op jit(solution)/shard_map/ppermute | solution.py:30
  44.3 0.2 maximum_maximum_fusion
  44.5 3.0 %subtract_bitcast_fusion.5 = (f32[1,8,1024]{2,1,0:T(8,128)S(1)}, f32[8,1024]{1,0:T(8,128)S(1)}, f32[8,1024]{1,0:T(8,128)S(1)}, f32[8,1024]{1,0:T(8,128)S(1)}, f3...) fusion(f32[8,1024]{1,0:T(8,128)S(1)} %get-tuple-element.86, ...), kind=kLoop, calls=%fused_computation.2557 | loop fusion | flops 9281536 | bytes 8728576 | tf_op jit(solution)/shard_map/stack | solution.py:81
  47.5 1.3 %subtract_bitcast_fusion.4 = f32[1,8,1024]{2,1,0:T(8,128)S(1)} fusion(f32[8,1024]{1,0:T(8,128)S(1)} %get-tuple-element.76, f32[8,1024]{1,0:T(8,128)S(1)} %get-tuple-element.75, f32[8,1024]{1,0:T(8,128)S(1)} %get-tuple-element.74, f32[8,1024]{1,0:T(8,128)S(1)} %get-tuple-element.73, f32[8,1024]{1,0:T(8,128)S(1)} %get-tuple-element.72, ...), kind=kLoop, calls=%fused_computation.2556 | loop fusion | flops 3825664 | bytes 4816896 | tf_op jit(solution)/shard_map/stack | solution.py:81
  48.9 1.9 %collective-permute-start.7 = (f32[4,3,1024]{2,1,0:T(4,128)S(1)}, f32[4,3,1024]{2,1,0:T(4,128)S(1)}, u32[]{:S(2)}, u32[]{:S(2)}) collective-permute-start(f32[4,3,1024]{2,1,0:T(4,128)S(1)} %get-tuple-element.107), channel_id=1, source_target_pairs={{0,16},{16,32},{32,48},{48,64},{64,80},{80,96},{96,112},{112,128},... | collective-permute-start | bytes 147464 | tf_op jit(solution)/shard_map/ppermute | solution.py:27
  50.8 5.5 %collective-permute-start.8 = (f32[4,3,1024]{2,1,0:T(4,128)S(1)}, f32[4,3,1024]{2,1,0:T(4,128)S(1)}, u32[]{:S(2)}, u32[]{:S(2)}) collective-permute-start(f32[4,3,1024]{2,1,0:T(4,128)S(1)} %get-tuple-element.108), channel_id=1, source_target_pairs={{16,0},{32,16},{48,32},{64,48},{80,64},{96,80},{112,96},{128,112},... | collective-permute-start | bytes 147464 | tf_op jit(solution)/shard_map/ppermute | solution.py:30
  56.3 1.3 %collective-permute-done.8 = f32[4,3,1024]{2,1,0:T(4,128)S(1)} collective-permute-done((f32[4,3,1024]{2,1,0:T(4,128)S(1)}, f32[4,3,1024]{2,1,0:T(4,128)S(1)}, u32[]{:S(2)}, u32[]{:S(2)}) %collective-permute-start.8) | collective-permute-done | bytes 49184 | tf_op jit(solution)/shard_map/ppermute | solution.py:30
  57.6 0.1 pad_maximum_fusion.11
  57.7 3.0 %collective-permute-start.10 = (f32[4,14,3]{2,1,0:T(8,128)S(1)}, f32[4,14,3]{2,1,0:T(8,128)S(1)}, u32[]{:S(2)}, u32[]{:S(2)}) collective-permute-start(f32[4,14,3]{2,1,0:T(8,128)S(1)} %get-tuple-element.95), channel_id=1, source_target_pairs={{0,1},{1,2},{2,3},{3,4},{4,5},{5,6},{6,7},{7,8},{8,9},{9,10},{10,1... | collective-permute-start | bytes 2024 | tf_op jit(solution)/shard_map/ppermute | solution.py:27
  60.7 1.9 %collective-permute-start.9 = (f32[4,14,3]{2,1,0:T(8,128)S(1)}, f32[4,14,3]{2,1,0:T(8,128)S(1)}, u32[]{:S(2)}, u32[]{:S(2)}) collective-permute-start(f32[4,14,3]{2,1,0:T(8,128)S(1)} %get-tuple-element.96), channel_id=1, source_target_pairs={{1,0},{2,1},{3,2},{4,3},{5,4},{6,5},{7,6},{8,7},{9,8},{10,9},{11,1... | collective-permute-start | bytes 2024 | tf_op jit(solution)/shard_map/ppermute | solution.py:30
  62.7 0.1 maximum_maximum_fusion.3
  62.7 6.8 %collective-permute-done.9 = f32[4,14,3]{2,1,0:T(8,128)S(1)} collective-permute-done((f32[4,14,3]{2,1,0:T(8,128)S(1)}, f32[4,14,3]{2,1,0:T(8,128)S(1)}, u32[]{:S(2)}, u32[]{:S(2)}) %collective-permute-start.9) | collective-permute-done | bytes 704 | tf_op jit(solution)/shard_map/ppermute | solution.py:30
  69.6 0.2 maximum_maximum_fusion.1
  69.8 2.9 %subtract_bitcast_fusion.3 = (f32[1,8,1024]{2,1,0:T(8,128)S(1)}, f32[8,1024]{1,0:T(8,128)S(1)}, f32[8,1024]{1,0:T(8,128)S(1)}, f32[8,1024]{1,0:T(8,128)S(1)}, f3...) fusion(f32[4,14,1027]{2,1,0:T(8,128)S(1)} %get-tuple-element.94, ...), kind=kLoop, calls=%fused_computation.2507 | loop fusion | flops 9805824 | bytes 7647232 | tf_op jit(solution)/shard_map/stack | solution.py:81
  72.7 2.6 %subtract_bitcast_fusion.2 = f32[1,8,1024]{2,1,0:T(8,128)S(1)} fusion(f32[8,1024]{1,0:T(8,128)S(1)} %get-tuple-element.25, f32[8,1024]{1,0:T(8,128)S(1)} %get-tuple-element.24, f32[8,1024]{1,0:T(8,128)S(1)} %get-tuple-element.23, f32[8,1024]{1,0:T(8,128)S(1)} %get-tuple-element.22, f32[8,1024]{1,0:T(8,128)S(1)} %get-tuple-element.21, ...), kind=kLoop, calls=%fused_computation.2506 | loop fusion | flops 8601600 | bytes 6815744 | tf_op jit(solution)/shard_map/stack | solution.py:81
  75.3 0.0 copy-start.3
  75.3 1.9 %collective-permute-start.11 = (f32[4,3,1024]{2,1,0:T(4,128)S(1)}, f32[4,3,1024]{2,1,0:T(4,128)S(1)}, u32[]{:S(2)}, u32[]{:S(2)}) collective-permute-start(f32[4,3,1024]{2,1,0:T(4,128)S(1)} %get-tuple-element.103), channel_id=1, source_target_pairs={{0,16},{16,32},{32,48},{48,64},{64,80},{80,96},{96,112},{112,128},... | collective-permute-start | bytes 147464 | tf_op jit(solution)/shard_map/ppermute | solution.py:27
  77.2 5.5 %collective-permute-start.12 = (f32[4,3,1024]{2,1,0:T(4,128)S(1)}, f32[4,3,1024]{2,1,0:T(4,128)S(1)}, u32[]{:S(2)}, u32[]{:S(2)}) collective-permute-start(f32[4,3,1024]{2,1,0:T(4,128)S(1)} %get-tuple-element.104), channel_id=1, source_target_pairs={{16,0},{32,16},{48,32},{64,48},{80,64},{96,80},{112,96},{128,112},... | collective-permute-start | bytes 147464 | tf_op jit(solution)/shard_map/ppermute | solution.py:30
  82.8 1.3 %collective-permute-done.12 = f32[4,3,1024]{2,1,0:T(4,128)S(1)} collective-permute-done((f32[4,3,1024]{2,1,0:T(4,128)S(1)}, f32[4,3,1024]{2,1,0:T(4,128)S(1)}, u32[]{:S(2)}, u32[]{:S(2)}) %collective-permute-start.12) | collective-permute-done | bytes 49184 | tf_op jit(solution)/shard_map/ppermute | solution.py:30
  84.1 0.1 pad_maximum_fusion.7
  84.1 3.4 %collective-permute-start.14 = (f32[4,14,3]{2,1,0:T(8,128)S(1)}, f32[4,14,3]{2,1,0:T(8,128)S(1)}, u32[]{:S(2)}, u32[]{:S(2)}) collective-permute-start(f32[4,14,3]{2,1,0:T(8,128)S(1)} %get-tuple-element.91), channel_id=1, source_target_pairs={{0,1},{1,2},{2,3},{3,4},{4,5},{5,6},{6,7},{7,8},{8,9},{9,10},{10,1... | collective-permute-start | bytes 2024 | tf_op jit(solution)/shard_map/ppermute | solution.py:27
  87.5 1.9 %collective-permute-start.13 = (f32[4,14,3]{2,1,0:T(8,128)S(1)}, f32[4,14,3]{2,1,0:T(8,128)S(1)}, u32[]{:S(2)}, u32[]{:S(2)}) collective-permute-start(f32[4,14,3]{2,1,0:T(8,128)S(1)} %get-tuple-element.92), channel_id=1, source_target_pairs={{1,0},{2,1},{3,2},{4,3},{5,4},{6,5},{7,6},{8,7},{9,8},{10,9},{11,1... | collective-permute-start | bytes 2024 | tf_op jit(solution)/shard_map/ppermute | solution.py:30
  89.5 0.1 maximum_maximum_fusion.4
  89.5 6.8 %collective-permute-done.13 = f32[4,14,3]{2,1,0:T(8,128)S(1)} collective-permute-done((f32[4,14,3]{2,1,0:T(8,128)S(1)}, f32[4,14,3]{2,1,0:T(8,128)S(1)}, u32[]{:S(2)}, u32[]{:S(2)}) %collective-permute-start.13) | collective-permute-done | bytes 704 | tf_op jit(solution)/shard_map/ppermute | solution.py:30
  96.4 0.2 maximum_maximum_fusion.2
  96.6 2.9 %subtract_bitcast_fusion.1 = (f32[1,8,1024]{2,1,0:T(8,128)S(1)}, f32[8,1024]{1,0:T(8,128)S(1)}, f32[8,1024]{1,0:T(8,128)S(1)}, f32[8,1024]{1,0:T(8,128)S(1)}, f3...) fusion(f32[4,14,1027]{2,1,0:T(8,128)S(1)} %get-tuple-element.90, ...), kind=kLoop, calls=%fused_computation.2457 | loop fusion | flops 9805824 | bytes 7647232 | tf_op jit(solution)/shard_map/stack | solution.py:81
  99.5 2.6 %subtract_bitcast_fusion = f32[1,8,1024]{2,1,0:T(8,128)S(1)} fusion(f32[8,1024]{1,0:T(8,128)S(1)} %get-tuple-element.12, f32[8,1024]{1,0:T(8,128)S(1)} %get-tuple-element.11, f32[8,1024]{1,0:T(8,128)S(1)} %get-tuple-element.10, f32[8,1024]{1,0:T(8,128)S(1)} %get-tuple-element.9, f32[8,1024]{1,0:T(8,128)S(1)} %get-tuple-element.8, ...), kind=kLoop, calls=%fused_computation.2456 | loop fusion | flops 8601600 | bytes 6815744 | tf_op jit(solution)/shard_map/stack | solution.py:81
  102.0 0.6 fusion.3
  (21 shorter events, 0.2 us)
Async XLA Ops:
  0.6 4.2 %copy-start.1 = (f32[2,8,1024]{2,1,0:T(8,128)S(1)}, f32[2,8,1024]{2,1,0:T(8,128)}, u32[]{:S(2)}) copy-start(f32[2,8,1024]{2,1,0:T(8,128)} %param.3) | copy-start | bytes 196612
  1.5 3.3 %copy-start.2 = (f32[2,8,1024]{2,1,0:T(8,128)S(1)}, f32[2,8,1024]{2,1,0:T(8,128)}, u32[]{:S(2)}) copy-start(f32[2,8,1024]{2,1,0:T(8,128)} %param.4) | copy-start | bytes 196612
  1.5 14.4 %collective-permute-start.3 = (s32[3,1024]{1,0:T(4,128)S(1)}, s32[3,1024]{1,0:T(4,128)S(1)}, u32[]{:S(2)}, u32[]{:S(2)}) collective-permute-start(s32[3,1024]{1,0:T(4,128)S(1)} %slice_bitcast_fusion), channel_id=1, source_target_pairs={{0,16},{16,32},{32,48},{48,64},{64,80},{80,96},{96,112},{112,128},... | collective-permute-start | bytes 36872 | tf_op jit(solution)/shard_map/ppermute | solution.py:37
  4.8 11.0 %copy-start = (s32[4,8,1024]{2,1,0:T(8,128)S(1)}, s32[4,8,1024]{2,1,0:T(8,128)}, u32[]{:S(2)}) copy-start(s32[4,8,1024]{2,1,0:T(8,128)} %param.5) | copy-start | bytes 393220
  4.9 22.3 %collective-permute-start.1 = (f32[4,3,1024]{2,1,0:T(4,128)S(1)}, f32[4,3,1024]{2,1,0:T(4,128)S(1)}, u32[]{:S(2)}, u32[]{:S(2)}) collective-permute-start(f32[4,3,1024]{2,1,0:T(4,128)S(1)} %get-tuple-element.109), channel_id=1, source_target_pairs={{16,0},{32,16},{48,32},{64,48},{80,64},{96,80},{112,96},{128,112},... | collective-permute-start | bytes 147464 | tf_op jit(solution)/shard_map/ppermute | solution.py:30
  16.0 11.1 %collective-permute-start.6 = (s32[11,3]{1,0:T(8,128)S(1)}, s32[11,3]{1,0:T(8,128)S(1)}, u32[]{:S(2)}, u32[]{:S(2)}) collective-permute-start(s32[11,3]{1,0:T(8,128)S(1)} %get-tuple-element.113), channel_id=1, source_target_pairs={{1,0},{2,1},{3,2},{4,3},{5,4},{6,5},{7,6},{8,7},{9,8},{10,9},{11,1... | collective-permute-start | bytes 404 | tf_op jit(solution)/shard_map/ppermute | solution.py:30
  18.8 8.3 %collective-permute-start.4 = (s32[11,3]{1,0:T(8,128)S(1)}, s32[11,3]{1,0:T(8,128)S(1)}, u32[]{:S(2)}, u32[]{:S(2)}) collective-permute-start(s32[11,3]{1,0:T(8,128)S(1)} %get-tuple-element.114), channel_id=1, source_target_pairs={{0,1},{1,2},{2,3},{3,4},{4,5},{5,6},{6,7},{7,8},{8,9},{9,10},{10,1... | collective-permute-start | bytes 404 | tf_op jit(solution)/shard_map/ppermute | solution.py:27
  25.2 7.1 %collective-permute-start = (f32[4,3,1024]{2,1,0:T(4,128)S(1)}, f32[4,3,1024]{2,1,0:T(4,128)S(1)}, u32[]{:S(2)}, u32[]{:S(2)}) collective-permute-start(f32[4,3,1024]{2,1,0:T(4,128)S(1)} %get-tuple-element.110), channel_id=1, source_target_pairs={{0,16},{16,32},{32,48},{48,64},{64,80},{80,96},{96,112},{112,128},... | collective-permute-start | bytes 147464 | tf_op jit(solution)/shard_map/ppermute | solution.py:27
  32.4 5.3 %collective-permute-start.5 = (f32[4,14,3]{2,1,0:T(8,128)S(1)}, f32[4,14,3]{2,1,0:T(8,128)S(1)}, u32[]{:S(2)}, u32[]{:S(2)}) collective-permute-start(f32[4,14,3]{2,1,0:T(8,128)S(1)} %get-tuple-element.99), channel_id=1, source_target_pairs={{0,1},{1,2},{2,3},{3,4},{4,5},{5,6},{6,7},{7,8},{8,9},{9,10},{10,1... | collective-permute-start | bytes 2024 | tf_op jit(solution)/shard_map/ppermute | solution.py:27
  35.5 8.8 %collective-permute-start.2 = (f32[4,14,3]{2,1,0:T(8,128)S(1)}, f32[4,14,3]{2,1,0:T(8,128)S(1)}, u32[]{:S(2)}, u32[]{:S(2)}) collective-permute-start(f32[4,14,3]{2,1,0:T(8,128)S(1)} %get-tuple-element.100), channel_id=1, source_target_pairs={{1,0},{2,1},{3,2},{4,3},{5,4},{6,5},{7,6},{8,7},{9,8},{10,9},{11,1... | collective-permute-start | bytes 2024 | tf_op jit(solution)/shard_map/ppermute | solution.py:30
  48.9 7.4 %collective-permute-start.7 = (f32[4,3,1024]{2,1,0:T(4,128)S(1)}, f32[4,3,1024]{2,1,0:T(4,128)S(1)}, u32[]{:S(2)}, u32[]{:S(2)}) collective-permute-start(f32[4,3,1024]{2,1,0:T(4,128)S(1)} %get-tuple-element.107), channel_id=1, source_target_pairs={{0,16},{16,32},{32,48},{48,64},{64,80},{80,96},{96,112},{112,128},... | collective-permute-start | bytes 147464 | tf_op jit(solution)/shard_map/ppermute | solution.py:27
  50.8 6.8 %collective-permute-start.8 = (f32[4,3,1024]{2,1,0:T(4,128)S(1)}, f32[4,3,1024]{2,1,0:T(4,128)S(1)}, u32[]{:S(2)}, u32[]{:S(2)}) collective-permute-start(f32[4,3,1024]{2,1,0:T(4,128)S(1)} %get-tuple-element.108), channel_id=1, source_target_pairs={{16,0},{32,16},{48,32},{64,48},{80,64},{96,80},{112,96},{128,112},... | collective-permute-start | bytes 147464 | tf_op jit(solution)/shard_map/ppermute | solution.py:30
  57.7 5.0 %collective-permute-start.10 = (f32[4,14,3]{2,1,0:T(8,128)S(1)}, f32[4,14,3]{2,1,0:T(8,128)S(1)}, u32[]{:S(2)}, u32[]{:S(2)}) collective-permute-start(f32[4,14,3]{2,1,0:T(8,128)S(1)} %get-tuple-element.95), channel_id=1, source_target_pairs={{0,1},{1,2},{2,3},{3,4},{4,5},{5,6},{6,7},{7,8},{8,9},{9,10},{10,1... | collective-permute-start | bytes 2024 | tf_op jit(solution)/shard_map/ppermute | solution.py:27
  60.7 8.8 %collective-permute-start.9 = (f32[4,14,3]{2,1,0:T(8,128)S(1)}, f32[4,14,3]{2,1,0:T(8,128)S(1)}, u32[]{:S(2)}, u32[]{:S(2)}) collective-permute-start(f32[4,14,3]{2,1,0:T(8,128)S(1)} %get-tuple-element.96), channel_id=1, source_target_pairs={{1,0},{2,1},{3,2},{4,3},{5,4},{6,5},{7,6},{8,7},{9,8},{10,9},{11,1... | collective-permute-start | bytes 2024 | tf_op jit(solution)/shard_map/ppermute | solution.py:30
  75.3 24.2 %copy-start.3 = (f32[2,8,1024]{2,1,0:T(8,128)}, f32[2,8,1024]{2,1,0:T(8,128)S(1)}, u32[]{:S(2)}) copy-start(f32[2,8,1024]{2,1,0:T(8,128)S(1)} %get-tuple-element.13) | copy-start | bytes 196612
  75.3 7.4 %collective-permute-start.11 = (f32[4,3,1024]{2,1,0:T(4,128)S(1)}, f32[4,3,1024]{2,1,0:T(4,128)S(1)}, u32[]{:S(2)}, u32[]{:S(2)}) collective-permute-start(f32[4,3,1024]{2,1,0:T(4,128)S(1)} %get-tuple-element.103), channel_id=1, source_target_pairs={{0,16},{16,32},{32,48},{48,64},{64,80},{80,96},{96,112},{112,128},... | collective-permute-start | bytes 147464 | tf_op jit(solution)/shard_map/ppermute | solution.py:27
  77.2 6.8 %collective-permute-start.12 = (f32[4,3,1024]{2,1,0:T(4,128)S(1)}, f32[4,3,1024]{2,1,0:T(4,128)S(1)}, u32[]{:S(2)}, u32[]{:S(2)}) collective-permute-start(f32[4,3,1024]{2,1,0:T(4,128)S(1)} %get-tuple-element.104), channel_id=1, source_target_pairs={{16,0},{32,16},{48,32},{64,48},{80,64},{96,80},{112,96},{128,112},... | collective-permute-start | bytes 147464 | tf_op jit(solution)/shard_map/ppermute | solution.py:30
  84.1 5.4 %collective-permute-start.14 = (f32[4,14,3]{2,1,0:T(8,128)S(1)}, f32[4,14,3]{2,1,0:T(8,128)S(1)}, u32[]{:S(2)}, u32[]{:S(2)}) collective-permute-start(f32[4,14,3]{2,1,0:T(8,128)S(1)} %get-tuple-element.91), channel_id=1, source_target_pairs={{0,1},{1,2},{2,3},{3,4},{4,5},{5,6},{6,7},{7,8},{8,9},{9,10},{10,1... | collective-permute-start | bytes 2024 | tf_op jit(solution)/shard_map/ppermute | solution.py:27
  87.5 8.8 %collective-permute-start.13 = (f32[4,14,3]{2,1,0:T(8,128)S(1)}, f32[4,14,3]{2,1,0:T(8,128)S(1)}, u32[]{:S(2)}, u32[]{:S(2)}) collective-permute-start(f32[4,14,3]{2,1,0:T(8,128)S(1)} %get-tuple-element.92), channel_id=1, source_target_pairs={{1,0},{2,1},{3,2},{4,3},{5,4},{6,5},{7,6},{8,7},{9,8},{10,9},{11,1... | collective-permute-start | bytes 2024 | tf_op jit(solution)/shard_map/ppermute | solution.py:30
where the time goes:
time: 103 us
  starting transfers between devices  55.4 us (54%)
  waiting for transfers between devices  28 us (27%)
  other arithmetic  18.2 us (18%)
  between operations  1.07 us (1%)
    ppermute x7, starting transfers between devices, extended(): lax.ppermute(lax.slice_in_dim(block, 0, width, axis=dim), axis, backward)  30.6 us
    ppermute x7, waiting for transfers between devices, extended(): lax.ppermute(lax.slice_in_dim(block, 0, width, axis=dim), axis, backward)  22.9 us
    ppermute x7, starting transfers between devices, extended(): lax.ppermute(lax.slice_in_dim(block, block.shape[dim] - width, None, axis...  21.6 us
    another operation x6, other arithmetic, twice_force(): return jnp.stack([force_x, force_y])  15.1 us
    ppermute x7, waiting for transfers between devices, extended(): lax.ppermute(lax.slice_in_dim(block, block.shape[dim] - width, None, axis...  5.08 us
    ppermute x1, starting transfers between devices, passed_along(): lax.ppermute(array, axis, [(i, (i + by) % devices) for i in range(devices)])  3.25 us
  transfers between devices with their start and end apart: 15, of which 6 were waited for; matrix products, arithmetic and copies ran while one was open for 1% of the time, Pallas kernels for 0%

commit v1 on v0

v1 whole, which is shorter than its diff:
```python
import math

import jax
import jax.numpy as jnp
from jax import lax
from jax.experimental import pallas as pl
from jax.experimental.pallas import tpu as pltpu
from jax.sharding import PartitionSpec as P

STIFFNESS = 40.0
TIME_STEP = 0.05
SOFTENING = 0.0625
PACK_SHIFT = (0, 3, 10, 17)
LANES = 128

ROWS = 8
PITCH = 9
BLOCK = ROWS * PITCH
FIELDS = 5
HALO = 9
GUARD = 8
LINES = 256


def row_line(row):
    return GUARD + PITCH * (row + HALO)


def lane_ids():
    return lax.broadcasted_iota(jnp.int32, (8, LANES), 1)


def pack_kernel(disp_ref, vel_ref, bonds_ref, edge_ref, block_ref):
    low_half = lane_ids() < LANES // 2
    for field in range(FIELDS):
        tiles = []
        for tile in range(ROWS):
            cols = pl.ds(tile * LANES, LANES)
            if field < 2:
                value = disp_ref[field, :, cols]
            elif field < 4:
                value = vel_ref[field - 2, :, cols]
            else:
                value = bonds_ref[0, :, cols]
                for word in (1, 2, 3):
                    value = value + bonds_ref[word, :, cols] * (1 << PACK_SHIFT[word])
                value = value.astype(jnp.float32)
            block_ref[pl.ds(field * BLOCK + tile + 1, ROWS, stride=PITCH), :] = value
            tiles.append(value)
        edge = jnp.where(low_half, tiles[0], tiles[-1])
        edge_ref[pl.ds(8 * field, 8), :] = edge
        block_ref[pl.ds(field * BLOCK, ROWS, stride=PITCH), :] = edge


def halo_kernel(parity_ref, block_in, even_ref, odd_ref, block_ref, first_ref, last_ref):
    low_half = lane_ids() < LANES // 2
    is_even = parity_ref[1] == 0
    block_ref[...] = block_in[...]
    for field in range(FIELDS):
        even = even_ref[pl.ds(8 * field, 8), :]
        odd = odd_ref[pl.ds(8 * field, 8), :]
        from_right = jnp.where(is_even, even, odd)
        from_left = jnp.where(is_even, odd, even)
        block_ref[pl.ds(field * BLOCK, ROWS, stride=PITCH), :] = jnp.where(
            low_half, from_right, from_left
        )
        first_ref[pl.ds(PITCH * field, PITCH), :] = block_ref[pl.ds(field * BLOCK, PITCH), :]
        last_ref[pl.ds(PITCH * field, PITCH), :] = block_ref[
            pl.ds(field * BLOCK + BLOCK - PITCH, PITCH), :
        ]


def shifted(here, after, before, by, lanes):
    if by > 0:
        return pltpu.roll(jnp.where(lanes < by, after, here), LANES - by, 1)
    if by < 0:
        return pltpu.roll(jnp.where(lanes >= LANES + by, before, here), -by, 1)
    return here


def force_lines(data, masks, push, pull, start, count, fresh_masks):
    lanes = lane_ids()

    def body(step, carry):
        line = start + 8 * step

        def at(field, offset):
            return data[field, pl.ds(line + offset, 8), :]

        here = [at(f, 0) for f in range(4)]
        after = [at(f, 1) for f in range(4)]
        before = [at(f, -1) for f in range(4)]
        near = []
        words = []
        for row_off in range(4):
            if row_off == 0:
                near.append(here)
            else:
                value = [at(f, -PITCH * row_off) for f in range(4)]
                value[0] = value[0] - float(row_off)
                near.append(value)
            if fresh_masks:
                words.append(at(4, -PITCH * row_off).astype(jnp.int32))
        own = [None] * 4
        for col_off in range(-3, 4):
            far = [shifted(here[f], after[f], before[f], col_off, lanes) for f in range(4)]
            if col_off:
                far[1] = far[1] + float(col_off)
            sum_x = sum_y = None
            for row_off in range(4):
                if row_off == 0 and col_off <= 0:
                    continue
                bit = col_off - 1 if row_off == 0 else col_off + 3
                slot = PACK_SHIFT[row_off] + bit
                squared = row_off * row_off + col_off * col_off
                rest = math.sqrt(squared + SOFTENING)
                base = near[row_off]
                along_x = far[0] - base[0]
                along_y = far[1] - base[1]
                rate_x = far[2] - base[2]
                rate_y = far[3] - base[3]
                inverse = lax.rsqrt(along_x * along_x + (along_y * along_y + SOFTENING))
                dot = along_x * rate_x + along_y * rate_y
                if fresh_masks:
                    mask = jnp.where((words[row_off] & (1 << slot)) != 0, 1.0 / squared, 0.0)
                    masks[slot, pl.ds(line, 8), :] = mask
                else:
                    mask = masks[slot, pl.ds(line, 8), :]
                scale = mask * (
                    STIFFNESS - (STIFFNESS * rest - dot * inverse) * inverse
                )
                pull_x = scale * along_x
                pull_y = scale * along_y
                sum_x = pull_x if sum_x is None else sum_x + pull_x
                sum_y = pull_y if sum_y is None else sum_y + pull_y
                if own[row_off] is None:
                    own[row_off] = (pull_x, pull_y)
                else:
                    own[row_off] = (own[row_off][0] + pull_x, own[row_off][1] + pull_y)
            push[2 * (col_off + 3), pl.ds(line, 8), :] = sum_x
            push[2 * (col_off + 3) + 1, pl.ds(line, 8), :] = sum_y
        for row_off in range(4):
            pull[2 * row_off, pl.ds(line, 8), :] = own[row_off][0]
            pull[2 * row_off + 1, pl.ds(line, 8), :] = own[row_off][1]
        return carry

    lax.fori_loop(0, count, body, 0)


def update_lines(data, push, pull, start, count, which):
    lanes = lane_ids()

    def body(step, carry):
        line = start + 8 * step
        for part in range(2):
            force = pull[part, pl.ds(line, 8), :]
            for row_off in (1, 2, 3):
                force = force + pull[2 * row_off + part, pl.ds(line + PITCH * row_off, 8), :]
            for col_off in range(-3, 4):
                slot = 2 * (col_off + 3) + part
                here = push[slot, pl.ds(line, 8), :]
                if col_off > 0:
                    here = shifted(here, None, push[slot, pl.ds(line - 1, 8), :], -col_off, lanes)
                elif col_off < 0:
                    here = shifted(here, push[slot, pl.ds(line + 1, 8), :], None, -col_off, lanes)
                force = force - here
            change = (0.5 * TIME_STEP) * force
            speed = data[2 + part, pl.ds(line, 8), :] + change
            if which == 1:
                speed = speed + change
            data[2 + part, pl.ds(line, 8), :] = speed
            if which < 2:
                data[part, pl.ds(line, 8), :] = (
                    data[part, pl.ds(line, 8), :] + TIME_STEP * speed
                )
        return carry

    lax.fori_loop(0, count, body, 0)


def step_kernel(
    parity_ref, block_ref, even_ref, odd_ref, below_ref, above_ref,
    disp_ref, vel_ref, data, masks, push, pull,
):
    lanes = lane_ids()
    low_half = lanes < LANES // 2
    is_even = parity_ref[0] == 0
    even_line = jnp.where(is_even, row_line(8), row_line(-8))
    odd_line = jnp.where(is_even, row_line(-8), row_line(8))
    for field in range(FIELDS):
        for part in range(PITCH):
            source = pl.ds(field * BLOCK + 8 * part, 8)
            data[field, pl.ds(row_line(0) + 8 * part, 8), :] = block_ref[source, :]
            data[field, pl.ds(even_line + 8 * part, 8), :] = even_ref[source, :]
            data[field, pl.ds(odd_line + 8 * part, 8), :] = odd_ref[source, :]
        ends = pl.ds(PITCH * field, PITCH)
        data[field, pl.ds(row_line(-9), PITCH), :] = below_ref[ends, :]
        data[field, pl.ds(row_line(16), PITCH), :] = above_ref[ends, :]
    for field in range(FIELDS):
        lines = [
            (row_line(-8) + 8 * PITCH * k, 8 if k < 3 else 2) for k in range(4)
        ]
        joined = []
        for line, size in lines:
            own = data[field, pl.ds(line, size, stride=PITCH), :]
            ahead = data[field, pl.ds(line - PITCH, size, stride=PITCH), :]
            joined.append(jnp.where(low_half[:size], ahead, own))
        for (line, size), value in zip(lines, joined):
            data[field, pl.ds(line, size, stride=PITCH), :] = value
    for which in range(3):
        reach = 3 * (2 - which)
        low, high = -reach, ROWS + reach
        first, last = row_line(low), row_line(high + 3) + 1
        force_lines(data, masks, push, pull, first, -(-(last - first) // 8), which == 0)
        last = row_line(high) + 1
        update_lines(data, push, pull, first, -(-(last - first) // 8), which)
    for tile in range(ROWS):
        lines = pl.ds(row_line(0) + 1 + tile, ROWS, stride=PITCH)
        cols = pl.ds(tile * LANES, LANES)
        for part in range(2):
            disp_ref[part, :, cols] = data[part, lines, :]
            vel_ref[part, :, cols] = data[2 + part, lines, :]


def shift(array, axis, by):
    count = lax.axis_size(axis)
    return lax.ppermute(array, axis, [(i, (i + by) % count) for i in range(count)])


def swap(array, axis, odd):
    count = lax.axis_size(axis)
    pairs = []
    for i in range(odd, count + odd, 2):
        pairs += [(i % count, (i + 1) % count), ((i + 1) % count, i % count)]
    return lax.ppermute(array, axis, pairs)


VMEM = pl.BlockSpec(memory_space=pltpu.VMEM)
SMEM = pl.BlockSpec(memory_space=pltpu.SMEM)


def per_device(disp, vel, bonds):
    f32 = jnp.float32
    parity = jnp.stack([lax.axis_index("gx") % 2, lax.axis_index("gy") % 2]).astype(jnp.int32)
    edge, block = pl.pallas_call(
        pack_kernel,
        out_shape=(
            jax.ShapeDtypeStruct((8 * FIELDS, LANES), f32),
            jax.ShapeDtypeStruct((FIELDS * BLOCK, LANES), f32),
        ),
        in_specs=[VMEM] * 3,
        out_specs=(VMEM, VMEM),
        name="pack",
    )(disp, vel, bonds)
    odd_edge = swap(edge, "gy", 1)
    even_edge = swap(edge, "gy", 0)
    ends = jax.ShapeDtypeStruct((FIELDS * PITCH, LANES), f32)
    block, first, last = pl.pallas_call(
        halo_kernel,
        out_shape=(jax.ShapeDtypeStruct((FIELDS * BLOCK, LANES), f32), ends, ends),
        in_specs=[SMEM] + [VMEM] * 3,
        out_specs=(VMEM,) * 3,
        name="halo",
    )(parity, block, even_edge, odd_edge)
    odd_block = swap(block, "gx", 1)
    even_block = swap(block, "gx", 0)
    below = shift(last, "gx", 2)
    above = shift(first, "gx", -2)
    out = jax.ShapeDtypeStruct(disp.shape, f32)
    return pl.pallas_call(
        step_kernel,
        out_shape=(out, out),
        in_specs=[SMEM] + [VMEM] * 5,
        out_specs=(VMEM, VMEM),
        scratch_shapes=[
            pltpu.VMEM((FIELDS, LINES, LANES), f32),
            pltpu.VMEM((24, LINES, LANES), f32),
            pltpu.VMEM((14, LINES, LANES), f32),
            pltpu.VMEM((8, LINES, LANES), f32),
        ],
        compiler_params=pltpu.CompilerParams(vmem_limit_bytes=16 * 2**20),
        name="steps",
    )(parity, block, even_block, odd_block, below, above)


def solution(mesh):
    spec = P(None, "gx", "gy")
    return jax.shard_map(
        per_device,
        mesh=mesh,
        in_specs=(spec, spec, spec),
        out_specs=(spec, spec),
        check_vma=False,
    )
```

time: 103 us -> 52.3 us (0.51)
  the two profiles are of different devices: /device:TPU:25 before, /device:TPU:2 now
where the time goes in v1:
time: 52.3 us; the launch traced here: 51.9 us
  starting transfers between devices  29.6 us (57%)
  Pallas kernels  17 us (33%)
  waiting for transfers between devices  2.46 us (5%)
  local copies, waits for them, and re-layouts  1.52 us (3%)
  between operations  0.72 us (1%)
  other arithmetic  0.6 us (1%)
    ppermute x4, starting transfers between devices, swap(): return lax.ppermute(array, axis, pairs)  22.6 us
    pallas_call x1, Pallas kernels, per_device(): pl.pallas_call(step_kernel, out_shape=(out, out), in_specs=[SMEM] + [VMEM...  13.7 us
    ppermute x2, starting transfers between devices, shift(): lax.ppermute(array, axis, [(i, (i + by) % count) for i in range(count)])  7.05 us
    ppermute x2, waiting for transfers between devices, shift(): lax.ppermute(array, axis, [(i, (i + by) % count) for i in range(count)])  1.71 us
    pallas_call x1, Pallas kernels, per_device(): pl.pallas_call(pack_kernel, out_shape=(jax.ShapeDtypeStruct((8 * FIELDS,...  1.69 us
    pallas_call x1, Pallas kernels, per_device(): pl.pallas_call(halo_kernel, out_shape=(jax.ShapeDtypeStruct((FIELDS * BLO...  1.64 us
    unnamed x8, local copies, waits for them, and re-layouts  1.52 us
  transfers between devices with their start and end apart: 6, of which 4 were waited for; matrix products, arithmetic and copies ran while one was open for 1% of the time, Pallas kernels for 0%

profile of v1, /device:TPU:2, one launch (start us, length us, event | category | flops | bytes accessed | tf_op | source)
XLA Modules:
  0.0 51.9 jit_solution(17266469482369314233)
XLA Ops:
  0.6 1.7 %pack.1 = (f32[40,128]{1,0:T(8,128)}, f32[360,128]{1,0:T(8,128)}) custom-call(f32[2,8,1024]{2,1,0:T(8,128)} %disp_ref.1, f32[2,8,1024]{2,1,0:T(8,128)} %vel_ref.1, s32[4,8,1024]{2,1,0:T(8,128)} %bonds_ref.1), custom_call_target="tpu_custom_call" | custom-call | tf_op jit(solution)/shard_map/pack/pallas_call | solution.py:245
  2.3 5.9 %collective-permute-start.1 = (f32[40,128]{1,0:T(8,128)}, f32[40,128]{1,0:T(8,128)S(1)}, u32[]{:S(2)}, u32[]{:S(2)}) collective-permute-start(f32[40,128]{1,0:T(8,128)} %get-tuple-element.8), channel_id=1, source_target_pairs={{1,2},{2,1},{3,4},{4,3},{5,6},{6,5},{7,8},{8,7},{9,10},{10,9},{11,... | collective-permute-start | bytes 61448 | tf_op jit(solution)/shard_map/ppermute | solution.py:235
  8.2 1.9 %collective-permute-start = (f32[40,128]{1,0:T(8,128)}, f32[40,128]{1,0:T(8,128)S(1)}, u32[]{:S(2)}, u32[]{:S(2)}) collective-permute-start(f32[40,128]{1,0:T(8,128)} %get-tuple-element.8), channel_id=1, source_target_pairs={{0,1},{1,0},{2,3},{3,2},{4,5},{5,4},{6,7},{7,6},{8,9},{9,8},{10,11... | collective-permute-start | bytes 61448 | tf_op jit(solution)/shard_map/ppermute | solution.py:235
  10.2 0.6 %pad_add_fusion.parity_ref = s32[2]{0:T(128)} fusion(s32[1]{0:T(128)} %bitcast.1, s32[1]{0:T(128)} %bitcast), kind=kLoop, calls=%fused_computation | loop fusion | flops 2 | bytes 16 | tf_op jit(solution)/shard_map/stack | solution.py:244
  10.8 0.5 collective-permute-done.1.odd_ref
  11.2 0.0 copy-start.2
  11.2 0.3 collective-permute-done.even_ref
  11.5 0.0 copy-start.3
  11.5 0.3 copy-done.2
  11.8 0.3 copy-done.3
  12.1 1.6 %halo.1 = (f32[360,128]{1,0:T(8,128)}, f32[45,128]{1,0:T(8,128)}, f32[45,128]{1,0:T(8,128)}) custom-call(s32[2]{0:T(128)} %pad_add_fusion.parity_ref, f32[360,128]{1,0:T(8,128)} %get-tuple-element.7.block_in, f32[40,128]{1,0:T(8,128)} %copy-done.3, f32[40,128]{1,0:T(8,128)} %copy-done.2), custom_call_target="tpu_custom_call" | custom-call | tf_op jit(solution)/shard_map/halo/pallas_call | solution.py:258
  13.8 4.7 %collective-permute-start.3 = (f32[360,128]{1,0:T(8,128)}, f32[360,128]{1,0:T(8,128)S(1)}, u32[]{:S(2)}, u32[]{:S(2)}) collective-permute-start(f32[360,128]{1,0:T(8,128)} %get-tuple-element.9.block_ref), channel_id=1, source_target_pairs={{16,32},{32,16},{48,64},{64,48},{80,96},{96,80},{112,128},{128,112... | collective-permute-start | bytes 552968 | tf_op jit(solution)/shard_map/ppermute | solution.py:235
  18.5 10.1 %collective-permute-start.2 = (f32[360,128]{1,0:T(8,128)}, f32[360,128]{1,0:T(8,128)S(1)}, u32[]{:S(2)}, u32[]{:S(2)}) collective-permute-start(f32[360,128]{1,0:T(8,128)} %get-tuple-element.9.block_ref), channel_id=1, source_target_pairs={{0,16},{16,0},{32,48},{48,32},{64,80},{80,64},{96,112},{112,96},{1... | collective-permute-start | bytes 552968 | tf_op jit(solution)/shard_map/ppermute | solution.py:235
  28.5 0.0 copy-start.1
  28.6 1.9 %collective-permute-start.4 = (f32[45,128]{1,0:T(8,128)}, f32[45,128]{1,0:T(8,128)S(1)}, u32[]{:S(2)}, u32[]{:S(2)}) collective-permute-start(f32[45,128]{1,0:T(8,128)} %get-tuple-element.10), channel_id=1, source_target_pairs={{0,32},{16,48},{32,64},{48,80},{64,96},{80,112},{96,128},{112,144}... | collective-permute-start | bytes 69128 | tf_op jit(solution)/shard_map/ppermute | solution.py:227
  30.5 5.1 %collective-permute-start.5 = (f32[45,128]{1,0:T(8,128)}, f32[45,128]{1,0:T(8,128)S(1)}, u32[]{:S(2)}, u32[]{:S(2)}) collective-permute-start(f32[45,128]{1,0:T(8,128)} %get-tuple-element.11), channel_id=1, source_target_pairs={{0,480},{16,496},{32,0},{48,16},{64,32},{80,48},{96,64},{112,80},{... | collective-permute-start | bytes 69128 | tf_op jit(solution)/shard_map/ppermute | solution.py:227
  35.6 0.1 collective-permute-done.4.below_ref
  35.7 1.6 %collective-permute-done.5.above_ref = f32[45,128]{1,0:T(8,128)S(1)} collective-permute-done((f32[45,128]{1,0:T(8,128)}, f32[45,128]{1,0:T(8,128)S(1)}, u32[]{:S(2)}, u32[]{:S(2)}) %collective-permute-start.5) | collective-permute-done | bytes 23072 | tf_op jit(solution)/shard_map/ppermute | solution.py:227
  37.3 0.0 collective-permute-done.3.odd_ref
  37.3 0.0 collective-permute-done.2.even_ref
  37.3 0.0 copy-done.1
  37.3 0.0 copy-start
  37.4 0.9 %copy-done = f32[360,128]{1,0:T(8,128)S(1)} copy-done((f32[360,128]{1,0:T(8,128)S(1)}, f32[360,128]{1,0:T(8,128)}, u32[]{:S(2)}) %copy-start) | copy-done | bytes 184344
  38.3 13.7 %steps.1 = (f32[2,8,1024]{2,1,0:T(8,128)}, f32[2,8,1024]{2,1,0:T(8,128)}) custom-call(s32[2]{0:T(128)S(1)} %copy-done.1, f32[360,128]{1,0:T(8,128)S(1)} %copy-done, f32[360,128]{1,0:T(8,128)S(1)} %collective-permute-done.2.even_ref, f32[360,128]{1,0:T(8,128)S(1)} %collective-permute-done.3.odd_ref, f32[45,128]{1,0:T(8,128)S(1)} %collective-permute-done.4.below_ref, ...), custom_call_target="tpu_custom_call" | custom-call | tf_op jit(solution)/shard_map/steps/pallas_call | solution.py:270
Async XLA Ops:
  2.3 8.9 %collective-permute-start.1 = (f32[40,128]{1,0:T(8,128)}, f32[40,128]{1,0:T(8,128)S(1)}, u32[]{:S(2)}, u32[]{:S(2)}) collective-permute-start(f32[40,128]{1,0:T(8,128)} %get-tuple-element.8), channel_id=1, source_target_pairs={{1,2},{2,1},{3,4},{4,3},{5,6},{6,5},{7,8},{8,7},{9,10},{10,9},{11,... | collective-permute-start | bytes 61448 | tf_op jit(solution)/shard_map/ppermute | solution.py:235
  8.2 3.3 %collective-permute-start = (f32[40,128]{1,0:T(8,128)}, f32[40,128]{1,0:T(8,128)S(1)}, u32[]{:S(2)}, u32[]{:S(2)}) collective-permute-start(f32[40,128]{1,0:T(8,128)} %get-tuple-element.8), channel_id=1, source_target_pairs={{0,1},{1,0},{2,3},{3,2},{4,5},{5,4},{6,7},{7,6},{8,9},{9,8},{10,11... | collective-permute-start | bytes 61448 | tf_op jit(solution)/shard_map/ppermute | solution.py:235
  11.2 0.6 %copy-start.2 = (f32[40,128]{1,0:T(8,128)}, f32[40,128]{1,0:T(8,128)S(1)}, u32[]{:S(2)}) copy-start(f32[40,128]{1,0:T(8,128)S(1)} %collective-permute-done.1.odd_ref) | copy-start | bytes 61444
  11.5 0.6 %copy-start.3 = (f32[40,128]{1,0:T(8,128)}, f32[40,128]{1,0:T(8,128)S(1)}, u32[]{:S(2)}) copy-start(f32[40,128]{1,0:T(8,128)S(1)} %collective-permute-done.even_ref) | copy-start | bytes 61444
  13.8 23.6 %collective-permute-start.3 = (f32[360,128]{1,0:T(8,128)}, f32[360,128]{1,0:T(8,128)S(1)}, u32[]{:S(2)}, u32[]{:S(2)}) collective-permute-start(f32[360,128]{1,0:T(8,128)} %get-tuple-element.9.block_ref), channel_id=1, source_target_pairs={{16,32},{32,16},{48,64},{64,48},{80,96},{96,80},{112,128},{128,112... | collective-permute-start | bytes 552968 | tf_op jit(solution)/shard_map/ppermute | solution.py:235
  18.5 18.9 %collective-permute-start.2 = (f32[360,128]{1,0:T(8,128)}, f32[360,128]{1,0:T(8,128)S(1)}, u32[]{:S(2)}, u32[]{:S(2)}) collective-permute-start(f32[360,128]{1,0:T(8,128)} %get-tuple-element.9.block_ref), channel_id=1, source_target_pairs={{0,16},{16,0},{32,48},{48,32},{64,80},{80,64},{96,112},{112,96},{1... | collective-permute-start | bytes 552968 | tf_op jit(solution)/shard_map/ppermute | solution.py:235
  28.5 8.8 %copy-start.1 = (s32[2]{0:T(128)S(1)}, s32[2]{0:T(128)}, u32[]{:S(2)}) copy-start(s32[2]{0:T(128)} %pad_add_fusion.parity_ref) | copy-start | bytes 28
  28.6 7.1 %collective-permute-start.4 = (f32[45,128]{1,0:T(8,128)}, f32[45,128]{1,0:T(8,128)S(1)}, u32[]{:S(2)}, u32[]{:S(2)}) collective-permute-start(f32[45,128]{1,0:T(8,128)} %get-tuple-element.10), channel_id=1, source_target_pairs={{0,32},{16,48},{32,64},{48,80},{64,96},{80,112},{96,128},{112,144}... | collective-permute-start | bytes 69128 | tf_op jit(solution)/shard_map/ppermute | solution.py:227
  30.5 6.8 %collective-permute-start.5 = (f32[45,128]{1,0:T(8,128)}, f32[45,128]{1,0:T(8,128)S(1)}, u32[]{:S(2)}, u32[]{:S(2)}) collective-permute-start(f32[45,128]{1,0:T(8,128)} %get-tuple-element.11), channel_id=1, source_target_pairs={{0,480},{16,496},{32,0},{48,16},{64,32},{80,48},{96,64},{112,80},{... | collective-permute-start | bytes 69128 | tf_op jit(solution)/shard_map/ppermute | solution.py:227
  37.3 0.9 %copy-start = (f32[360,128]{1,0:T(8,128)S(1)}, f32[360,128]{1,0:T(8,128)}, u32[]{:S(2)}) copy-start(f32[360,128]{1,0:T(8,128)} %get-tuple-element.9.block_ref) | copy-start | bytes 552964

commit v2 on v1

--- a/solution.py
+++ b/solution.py
@@ -30,44 +30,56 @@
     return lax.broadcasted_iota(jnp.int32, (8, LANES), 1)
 
 
-def pack_kernel(disp_ref, vel_ref, bonds_ref, edge_ref, block_ref):
+def edge_kernel(disp_hbm, vel_hbm, bonds_hbm, edge_ref, disp, vel, bonds, sems):
+    copies = []
+    for side in range(2):
+        cols = pl.ds(side * (ROWS - 1) * LANES, LANES)
+        for k, (source, target) in enumerate(
+            ((disp_hbm, disp), (vel_hbm, vel), (bonds_hbm, bonds))
+        ):
+            copies.append(
+                pltpu.make_async_copy(source.at[:, :, cols], target.at[side], sems.at[side, k])
+            )
+    for copy in copies:
+        copy.start()
+    for copy in copies:
+        copy.wait()
     low_half = lane_ids() < LANES // 2
-    for field in range(FIELDS):
-        tiles = []
-        for tile in range(ROWS):
-            cols = pl.ds(tile * LANES, LANES)
-            if field < 2:
-                value = disp_ref[field, :, cols]
-            elif field < 4:
-                value = vel_ref[field - 2, :, cols]
-            else:
-                value = bonds_ref[0, :, cols]
-                for word in (1, 2, 3):
-                    value = value + bonds_ref[word, :, cols] * (1 << PACK_SHIFT[word])
-                value = value.astype(jnp.float32)
-            block_ref[pl.ds(field * BLOCK + tile + 1, ROWS, stride=PITCH), :] = value
-            tiles.append(value)
-        edge = jnp.where(low_half, tiles[0], tiles[-1])
-        edge_ref[pl.ds(8 * field, 8), :] = edge
-        block_ref[pl.ds(field * BLOCK, ROWS, stride=PITCH), :] = edge
-
-
-def halo_kernel(parity_ref, block_in, even_ref, odd_ref, block_ref, first_ref, last_ref):
+    for part in range(2):
+        edge_ref[pl.ds(8 * part, 8), :] = jnp.where(low_half, disp[0, part], disp[1, part])
+        edge_ref[pl.ds(8 * part + 16, 8), :] = jnp.where(low_half, vel[0, part], vel[1, part])
+    words = [jnp.where(low_half, bonds[0, word], bonds[1, word]) for word in range(4)]
+    edge_ref[pl.ds(32, 8), :] = packed(words)
+
+
+def packed(words):
+    total = words[0]
+    for word in (1, 2, 3):
+        total = total + words[word] * (1 << PACK_SHIFT[word])
+    return total.astype(jnp.float32)
+
+
+def block_kernel(disp_ref, vel_ref, bonds_ref, even_ref, odd_ref, block_ref, first_ref, last_ref):
     low_half = lane_ids() < LANES // 2
-    is_even = parity_ref[1] == 0
-    block_ref[...] = block_in[...]
+    is_even = lax.rem(lax.axis_index("gy"), 2) == 0
     for field in range(FIELDS):
         even = even_ref[pl.ds(8 * field, 8), :]
         odd = odd_ref[pl.ds(8 * field, 8), :]
         from_right = jnp.where(is_even, even, odd)
         from_left = jnp.where(is_even, odd, even)
-        block_ref[pl.ds(field * BLOCK, ROWS, stride=PITCH), :] = jnp.where(
-            low_half, from_right, from_left
-        )
-        first_ref[pl.ds(PITCH * field, PITCH), :] = block_ref[pl.ds(field * BLOCK, PITCH), :]
-        last_ref[pl.ds(PITCH * field, PITCH), :] = block_ref[
-            pl.ds(field * BLOCK + BLOCK - PITCH, PITCH), :
-        ]
+        lines = [jnp.where(low_half, from_right, from_left)]
+        for tile in range(ROWS):
+            cols = pl.ds(tile * LANES, LANES)
+            if field < 2:
+                lines.append(disp_ref[field, :, cols])
+            elif field < 4:
+                lines.append(vel_ref[field - 2, :, cols])
+            else:
+                lines.append(packed([bonds_ref[word, :, cols] for word in range(4)]))
+        for k, value in enumerate(lines):
+            block_ref[pl.ds(field * BLOCK + k, ROWS, stride=PITCH), :] = value
+            first_ref[pl.ds(PITCH * field + k, 1), :] = value[:1]
+            last_ref[pl.ds(PITCH * field + k, 1), :] = value[7:]
 
 
 def shifted(here, after, before, by, lanes):
@@ -147,44 +159,50 @@
     lax.fori_loop(0, count, body, 0)
 
 
-def update_lines(data, push, pull, start, count, which):
+def update_lines(data, push, pull, start, count, which, unroll):
     lanes = lane_ids()
 
+    def change(line, part):
+        force = pull[part, pl.ds(line, 8), :]
+        for row_off in (1, 2, 3):
+            force = force + pull[2 * row_off + part, pl.ds(line + PITCH * row_off, 8), :]
+        for col_off in range(-3, 4):
+            slot = 2 * (col_off + 3) + part
+            here = push[slot, pl.ds(line, 8), :]
+            if col_off > 0:
+                here = shifted(here, None, push[slot, pl.ds(line - 1, 8), :], -col_off, lanes)
+            elif col_off < 0:
+                here = shifted(here, push[slot, pl.ds(line + 1, 8), :], None, -col_off, lanes)
+            force = force - here
+        return (0.5 * TIME_STEP) * force
+
     def body(step, carry):
-        line = start + 8 * step
-        for part in range(2):
-            force = pull[part, pl.ds(line, 8), :]
-            for row_off in (1, 2, 3):
-                force = force + pull[2 * row_off + part, pl.ds(line + PITCH * row_off, 8), :]
-            for col_off in range(-3, 4):
-                slot = 2 * (col_off + 3) + part
-                here = push[slot, pl.ds(line, 8), :]
-                if col_off > 0:
-                    here = shifted(here, None, push[slot, pl.ds(line - 1, 8), :], -col_off, lanes)
-                elif col_off < 0:
-                    here = shifted(here, push[slot, pl.ds(line + 1, 8), :], None, -col_off, lanes)
-                force = force - here
-            change = (0.5 * TIME_STEP) * force
-            speed = data[2 + part, pl.ds(line, 8), :] + change
-            if which == 1:
-                speed = speed + change
-            data[2 + part, pl.ds(line, 8), :] = speed
-            if which < 2:
-                data[part, pl.ds(line, 8), :] = (
-                    data[part, pl.ds(line, 8), :] + TIME_STEP * speed
-                )
+        base = start + 8 * unroll * step
+        stores = []
+        for line in [base + 8 * k for k in range(unroll)]:
+            for part in range(2):
+                gain = change(line, part)
+                speed = data[2 + part, pl.ds(line, 8), :] + gain
+                if which == 1:
+                    speed = speed + gain
+                stores.append((2 + part, line, speed))
+                if which < 2:
+                    moved = data[part, pl.ds(line, 8), :] + TIME_STEP * speed
+                    stores.append((part, line, moved))
+        for field, line, value in stores:
+            data[field, pl.ds(line, 8), :] = value
         return carry
 
-    lax.fori_loop(0, count, body, 0)
+    lax.fori_loop(0, -(-count // unroll), body, 0)
 
 
 def step_kernel(
-    parity_ref, block_ref, even_ref, odd_ref, below_ref, above_ref,
+    block_ref, even_ref, odd_ref, below_ref, above_ref,
     disp_ref, vel_ref, data, masks, push, pull,
 ):
     lanes = lane_ids()
     low_half = lanes < LANES // 2
-    is_even = parity_ref[0] == 0
+    is_even = lax.rem(lax.axis_index("gx"), 2) == 0
     even_line = jnp.where(is_even, row_line(8), row_line(-8))
     odd_line = jnp.where(is_even, row_line(-8), row_line(8))
     for field in range(FIELDS):
@@ -213,7 +231,7 @@
         first, last = row_line(low), row_line(high + 3) + 1
         force_lines(data, masks, push, pull, first, -(-(last - first) // 8), which == 0)
         last = row_line(high) + 1
-        update_lines(data, push, pull, first, -(-(last - first) // 8), which)
+        update_lines(data, push, pull, first, -(-(last - first) // 8), which, (4, 4, 3)[which])
     for tile in range(ROWS):
         lines = pl.ds(row_line(0) + 1 + tile, ROWS, stride=PITCH)
         cols = pl.ds(tile * LANES, LANES)
@@ -236,32 +254,36 @@
 
 
 VMEM = pl.BlockSpec(memory_space=pltpu.VMEM)
-SMEM = pl.BlockSpec(memory_space=pltpu.SMEM)
 
 
 def per_device(disp, vel, bonds):
     f32 = jnp.float32
-    parity = jnp.stack([lax.axis_index("gx") % 2, lax.axis_index("gy") % 2]).astype(jnp.int32)
-    edge, block = pl.pallas_call(
-        pack_kernel,
-        out_shape=(
-            jax.ShapeDtypeStruct((8 * FIELDS, LANES), f32),
-            jax.ShapeDtypeStruct((FIELDS * BLOCK, LANES), f32),
-        ),
-        in_specs=[VMEM] * 3,
-        out_specs=(VMEM, VMEM),
-        name="pack",
-    )(disp, vel, bonds)
+    small = pltpu.CompilerParams(vmem_limit_bytes=4 * 2**20)
+    edge = pl.pallas_call(
+        edge_kernel,
+        out_shape=jax.ShapeDtypeStruct((8 * FIELDS, LANES), f32),
+        in_specs=[pl.BlockSpec(memory_space=pltpu.HBM)] * 3,
+        out_specs=VMEM,
+        scratch_shapes=[
+            pltpu.VMEM((2, 2, ROWS, LANES), f32),
+            pltpu.VMEM((2, 2, ROWS, LANES), f32),
+            pltpu.VMEM((2, 4, ROWS, LANES), jnp.int32),
+            pltpu.SemaphoreType.DMA((2, 3)),
+        ],
+        compiler_params=small,
+        name="edge",
+    )(*(pltpu.with_memory_space_constraint(x, pltpu.HBM) for x in (disp, vel, bonds)))
     odd_edge = swap(edge, "gy", 1)
     even_edge = swap(edge, "gy", 0)
     ends = jax.ShapeDtypeStruct((FIELDS * PITCH, LANES), f32)
     block, first, last = pl.pallas_call(
-        halo_kernel,
+        block_kernel,
         out_shape=(jax.ShapeDtypeStruct((FIELDS * BLOCK, LANES), f32), ends, ends),
-        in_specs=[SMEM] + [VMEM] * 3,
+        in_specs=[VMEM] * 5,
         out_specs=(VMEM,) * 3,
-        name="halo",
-    )(parity, block, even_edge, odd_edge)
+        compiler_params=small,
+        name="block",
+    )(disp, vel, bonds, even_edge, odd_edge)
     odd_block = swap(block, "gx", 1)
     even_block = swap(block, "gx", 0)
     below = shift(last, "gx", 2)
@@ -270,7 +292,7 @@
     return pl.pallas_call(
         step_kernel,
         out_shape=(out, out),
-        in_specs=[SMEM] + [VMEM] * 5,
+        in_specs=[VMEM] * 5,
         out_specs=(VMEM, VMEM),
         scratch_shapes=[
             pltpu.VMEM((FIELDS, LINES, LANES), f32),
@@ -280,7 +302,7 @@
         ],
         compiler_params=pltpu.CompilerParams(vmem_limit_bytes=16 * 2**20),
         name="steps",
-    )(parity, block, even_block, odd_block, below, above)
+    )(block, even_block, odd_block, below, above)
 
 
 def solution(mesh):

time: 52.3 us -> 44.9 us (0.86)
  Pallas kernels: 17 us -> 11.5 us
  local copies, waits for them, and re-layouts: 1.52 us -> 0.01 us
  other arithmetic: 0.6 us -> 0 us
    pallas_call x3, Pallas kernels: 17 us -> 11.5 us  [the longest x1 10.6 us: per_device(): pl.pallas_call(step_kernel, out_shape=(out, out), in_specs=[VMEM] * 5, ou...]
    unnamed x8 -> x6, local copies, waits for them, and re-layouts: 1.52 us -> 0.01 us
    another operation x1 -> x0, other arithmetic: 0.6 us -> none  [per_device(): jnp.stack([lax.axis_index('gx') % 2, lax.axis_index('gy') % 2])]
  transfers between devices with their start and end apart: 6 -> 6, of which waited for: 4 -> 3; matrix products, arithmetic and copies ran while one was open for 1% -> 0% of each run, Pallas kernels for 0% -> 0%
where the time goes in v2:
time: 44.9 us; the launch traced here: 44.6 us
  starting transfers between devices  29.7 us (66%)
  Pallas kernels  11.5 us (26%)
  waiting for transfers between devices  2.65 us (6%)
  between operations  0.73 us (2%)
    ppermute x4, starting transfers between devices, swap(): return lax.ppermute(array, axis, pairs)  22.6 us
    pallas_call x1, Pallas kernels, per_device(): pl.pallas_call(step_kernel, out_shape=(out, out), in_specs=[VMEM] * 5, ou...  10.6 us
    ppermute x2, starting transfers between devices, shift(): lax.ppermute(array, axis, [(i, (i + by) % count) for i in range(count)])  7.05 us
    ppermute x2, waiting for transfers between devices, shift(): lax.ppermute(array, axis, [(i, (i + by) % count) for i in range(count)])  1.49 us
    ppermute x4, waiting for transfers between devices, swap(): return lax.ppermute(array, axis, pairs)  1.16 us
    pallas_call x1, Pallas kernels, per_device(): pl.pallas_call(edge_kernel, out_shape=jax.ShapeDtypeStruct((8 * FIELDS, L...  0.91 us
  transfers between devices with their start and end apart: 6, of which 3 were waited for; matrix products, arithmetic and copies ran while one was open for 0% of the time, Pallas kernels for 0%

profile of v2, /device:TPU:2, one launch (start us, length us, event | category | flops | bytes accessed | tf_op | source)
XLA Modules:
  0.0 44.6 jit_solution(17968905827020535910)
XLA Ops:
  0.6 0.0 copy-start
  0.6 0.0 copy-start.2
  0.6 0.0 copy-start.1
  0.7 0.9 %edge.1 = f32[40,128]{1,0:T(8,128)S(1)} custom-call(f32[2,8,1024]{2,1,0:T(8,128)} %disp_ref.1, f32[2,8,1024]{2,1,0:T(8,128)} %vel_ref.1, s32[4,8,1024]{2,1,0:T(8,128)} %bonds_ref.1), custom_call_target="tpu_custom_call" | custom-call | tf_op jit(solution)/shard_map/edge/pallas_call | solution.py:262
  1.6 5.9 %collective-permute-start.1 = (f32[40,128]{1,0:T(8,128)S(1)}, f32[40,128]{1,0:T(8,128)S(1)}, u32[]{:S(2)}, u32[]{:S(2)}) collective-permute-start(f32[40,128]{1,0:T(8,128)S(1)} %edge.1), channel_id=1, source_target_pairs={{1,2},{2,1},{3,4},{4,3},{5,6},{6,5},{7,8},{8,7},{9,10},{10,9},{11,... | collective-permute-start | bytes 61448 | tf_op jit(solution)/shard_map/ppermute | solution.py:253
  7.5 1.9 %collective-permute-start = (f32[40,128]{1,0:T(8,128)S(1)}, f32[40,128]{1,0:T(8,128)S(1)}, u32[]{:S(2)}, u32[]{:S(2)}) collective-permute-start(f32[40,128]{1,0:T(8,128)S(1)} %edge.1), channel_id=1, source_target_pairs={{0,1},{1,0},{2,3},{3,2},{4,5},{5,4},{6,7},{7,6},{8,9},{9,8},{10,11... | collective-permute-start | bytes 61448 | tf_op jit(solution)/shard_map/ppermute | solution.py:253
  9.4 0.9 %collective-permute-done.1.odd_ref = f32[40,128]{1,0:T(8,128)S(1)} collective-permute-done((f32[40,128]{1,0:T(8,128)S(1)}, f32[40,128]{1,0:T(8,128)S(1)}, u32[]{:S(2)}, u32[]{:S(2)}) %collective-permute-start.1) | collective-permute-done | bytes 20512 | tf_op jit(solution)/shard_map/ppermute | solution.py:253
  10.3 0.3 collective-permute-done.even_ref
  10.6 0.0 copy-done
  10.6 0.0 copy-done.2
  10.6 0.0 copy-done.1
  10.6 4.7 %collective-permute-start.3 = (f32[360,128]{1,0:T(8,128)S(1)}, f32[360,128]{1,0:T(8,128)S(1)}, u32[]{:S(2)}, u32[]{:S(2)}) collective-permute-start(f32[360,128]{1,0:T(8,128)S(1)} %get-tuple-element.5.block_ref), channel_id=1, source_target_pairs={{16,32},{32,16},{48,64},{64,48},{80,96},{96,80},{112,128},{128,112... | collective-permute-start | bytes 552968 | tf_op jit(solution)/shard_map/ppermute | solution.py:253
  15.3 10.1 %collective-permute-start.2 = (f32[360,128]{1,0:T(8,128)S(1)}, f32[360,128]{1,0:T(8,128)S(1)}, u32[]{:S(2)}, u32[]{:S(2)}) collective-permute-start(f32[360,128]{1,0:T(8,128)S(1)} %get-tuple-element.5.block_ref), channel_id=1, source_target_pairs={{0,16},{16,0},{32,48},{48,32},{64,80},{80,64},{96,112},{112,96},{1... | collective-permute-start | bytes 552968 | tf_op jit(solution)/shard_map/ppermute | solution.py:253
  25.4 1.9 %collective-permute-start.4 = (f32[45,128]{1,0:T(8,128)S(1)}, f32[45,128]{1,0:T(8,128)S(1)}, u32[]{:S(2)}, u32[]{:S(2)}) collective-permute-start(f32[45,128]{1,0:T(8,128)S(1)} %get-tuple-element.6), channel_id=1, source_target_pairs={{0,32},{16,48},{32,64},{48,80},{64,96},{80,112},{96,128},{112,144}... | collective-permute-start | bytes 69128 | tf_op jit(solution)/shard_map/ppermute | solution.py:245
  27.4 5.1 %collective-permute-start.5 = (f32[45,128]{1,0:T(8,128)S(1)}, f32[45,128]{1,0:T(8,128)S(1)}, u32[]{:S(2)}, u32[]{:S(2)}) collective-permute-start(f32[45,128]{1,0:T(8,128)S(1)} %get-tuple-element.7), channel_id=1, source_target_pairs={{0,480},{16,496},{32,0},{48,16},{64,32},{80,48},{96,64},{112,80},{... | collective-permute-start | bytes 69128 | tf_op jit(solution)/shard_map/ppermute | solution.py:245
  32.5 0.0 collective-permute-done.4.below_ref
  32.5 1.5 %collective-permute-done.5.above_ref = f32[45,128]{1,0:T(8,128)S(1)} collective-permute-done((f32[45,128]{1,0:T(8,128)S(1)}, f32[45,128]{1,0:T(8,128)S(1)}, u32[]{:S(2)}, u32[]{:S(2)}) %collective-permute-start.5) | collective-permute-done | bytes 23072 | tf_op jit(solution)/shard_map/ppermute | solution.py:245
  34.0 0.0 collective-permute-done.3.odd_ref
  34.0 0.0 collective-permute-done.2.even_ref
  34.0 10.6 %steps.1 = (f32[2,8,1024]{2,1,0:T(8,128)}, f32[2,8,1024]{2,1,0:T(8,128)}) custom-call(f32[360,128]{1,0:T(8,128)S(1)} %get-tuple-element.5.block_ref, f32[360,128]{1,0:T(8,128)S(1)} %collective-permute-done.2.even_ref, f32[360,128]{1,0:T(8,128)S(1)} %collective-permute-done.3.odd_ref, f32[45,128]{1,0:T(8,128)S(1)} %collective-permute-done.4.below_ref, ...), custom_call_target="tpu_custom_call" | custom-call | tf_op jit(solution)/shard_map/steps/pallas_call | solution.py:292
  (1 shorter events, 0.0 us)
Async XLA Ops:
  0.6 10.0 %copy-start = (s32[4,8,1024]{2,1,0:T(8,128)S(1)}, s32[4,8,1024]{2,1,0:T(8,128)}, u32[]{:S(2)}) copy-start(s32[4,8,1024]{2,1,0:T(8,128)} %bonds_ref.1) | copy-start | bytes 393220
  0.6 10.0 %copy-start.2 = (f32[2,8,1024]{2,1,0:T(8,128)S(1)}, f32[2,8,1024]{2,1,0:T(8,128)}, u32[]{:S(2)}) copy-start(f32[2,8,1024]{2,1,0:T(8,128)} %vel_ref.1) | copy-start | bytes 196612
  0.6 9.9 %copy-start.1 = (f32[2,8,1024]{2,1,0:T(8,128)S(1)}, f32[2,8,1024]{2,1,0:T(8,128)}, u32[]{:S(2)}) copy-start(f32[2,8,1024]{2,1,0:T(8,128)} %disp_ref.1) | copy-start | bytes 196612
  1.6 8.7 %collective-permute-start.1 = (f32[40,128]{1,0:T(8,128)S(1)}, f32[40,128]{1,0:T(8,128)S(1)}, u32[]{:S(2)}, u32[]{:S(2)}) collective-permute-start(f32[40,128]{1,0:T(8,128)S(1)} %edge.1), channel_id=1, source_target_pairs={{1,2},{2,1},{3,4},{4,3},{5,6},{6,5},{7,8},{8,7},{9,10},{10,9},{11,... | collective-permute-start | bytes 61448 | tf_op jit(solution)/shard_map/ppermute | solution.py:253
  7.5 3.1 %collective-permute-start = (f32[40,128]{1,0:T(8,128)S(1)}, f32[40,128]{1,0:T(8,128)S(1)}, u32[]{:S(2)}, u32[]{:S(2)}) collective-permute-start(f32[40,128]{1,0:T(8,128)S(1)} %edge.1), channel_id=1, source_target_pairs={{0,1},{1,0},{2,3},{3,2},{4,5},{5,4},{6,7},{7,6},{8,9},{9,8},{10,11... | collective-permute-start | bytes 61448 | tf_op jit(solution)/shard_map/ppermute | solution.py:253
  10.6 23.4 %collective-permute-start.3 = (f32[360,128]{1,0:T(8,128)S(1)}, f32[360,128]{1,0:T(8,128)S(1)}, u32[]{:S(2)}, u32[]{:S(2)}) collective-permute-start(f32[360,128]{1,0:T(8,128)S(1)} %get-tuple-element.5.block_ref), channel_id=1, source_target_pairs={{16,32},{32,16},{48,64},{64,48},{80,96},{96,80},{112,128},{128,112... | collective-permute-start | bytes 552968 | tf_op jit(solution)/shard_map/ppermute | solution.py:253
  15.3 18.7 %collective-permute-start.2 = (f32[360,128]{1,0:T(8,128)S(1)}, f32[360,128]{1,0:T(8,128)S(1)}, u32[]{:S(2)}, u32[]{:S(2)}) collective-permute-start(f32[360,128]{1,0:T(8,128)S(1)} %get-tuple-element.5.block_ref), channel_id=1, source_target_pairs={{0,16},{16,0},{32,48},{48,32},{64,80},{80,64},{96,112},{112,96},{1... | collective-permute-start | bytes 552968 | tf_op jit(solution)/shard_map/ppermute | solution.py:253
  25.4 7.1 %collective-permute-start.4 = (f32[45,128]{1,0:T(8,128)S(1)}, f32[45,128]{1,0:T(8,128)S(1)}, u32[]{:S(2)}, u32[]{:S(2)}) collective-permute-start(f32[45,128]{1,0:T(8,128)S(1)} %get-tuple-element.6), channel_id=1, source_target_pairs={{0,32},{16,48},{32,64},{48,80},{64,96},{80,112},{96,128},{112,144}... | collective-permute-start | bytes 69128 | tf_op jit(solution)/shard_map/ppermute | solution.py:245
  27.4 6.6 %collective-permute-start.5 = (f32[45,128]{1,0:T(8,128)S(1)}, f32[45,128]{1,0:T(8,128)S(1)}, u32[]{:S(2)}, u32[]{:S(2)}) collective-permute-start(f32[45,128]{1,0:T(8,128)S(1)} %get-tuple-element.7), channel_id=1, source_target_pairs={{0,480},{16,496},{32,0},{48,16},{64,32},{80,48},{96,64},{112,80},{... | collective-permute-start | bytes 69128 | tf_op jit(solution)/shard_map/ppermute | solution.py:245

commit v3 on v2

--- a/solution.py
+++ b/solution.py
@@ -31,25 +31,27 @@
 
 
 def edge_kernel(disp_hbm, vel_hbm, bonds_hbm, edge_ref, disp, vel, bonds, sems):
-    copies = []
-    for side in range(2):
-        cols = pl.ds(side * (ROWS - 1) * LANES, LANES)
+    copies = [
+        pltpu.make_async_copy(source, target, sems.at[k])
         for k, (source, target) in enumerate(
             ((disp_hbm, disp), (vel_hbm, vel), (bonds_hbm, bonds))
-        ):
-            copies.append(
-                pltpu.make_async_copy(source.at[:, :, cols], target.at[side], sems.at[side, k])
-            )
+        )
+    ]
     for copy in copies:
         copy.start()
     for copy in copies:
         copy.wait()
     low_half = lane_ids() < LANES // 2
+    left = pl.ds(0, LANES)
+    right = pl.ds((ROWS - 1) * LANES, LANES)
+
+    def ends(ref, part):
+        return jnp.where(low_half, ref[part, :, left], ref[part, :, right])
+
     for part in range(2):
-        edge_ref[pl.ds(8 * part, 8), :] = jnp.where(low_half, disp[0, part], disp[1, part])
-        edge_ref[pl.ds(8 * part + 16, 8), :] = jnp.where(low_half, vel[0, part], vel[1, part])
-    words = [jnp.where(low_half, bonds[0, word], bonds[1, word]) for word in range(4)]
-    edge_ref[pl.ds(32, 8), :] = packed(words)
+        edge_ref[pl.ds(8 * part, 8), :] = ends(disp, part)
+        edge_ref[pl.ds(8 * part + 16, 8), :] = ends(vel, part)
+    edge_ref[pl.ds(32, 8), :] = packed([ends(bonds, word) for word in range(4)])
 
 
 def packed(words):
@@ -114,11 +116,13 @@
             if fresh_masks:
                 words.append(at(4, -PITCH * row_off).astype(jnp.int32))
         own = [None] * 4
+        main = [None] * 2
+        carry_over = [None] * 2
         for col_off in range(-3, 4):
             far = [shifted(here[f], after[f], before[f], col_off, lanes) for f in range(4)]
             if col_off:
                 far[1] = far[1] + float(col_off)
-            sum_x = sum_y = None
+            sums = [None] * 2
             for row_off in range(4):
                 if row_off == 0 and col_off <= 0:
                     continue
@@ -138,43 +142,45 @@
                     masks[slot, pl.ds(line, 8), :] = mask
                 else:
                     mask = masks[slot, pl.ds(line, 8), :]
-                scale = mask * (
-                    STIFFNESS - (STIFFNESS * rest - dot * inverse) * inverse
-                )
-                pull_x = scale * along_x
-                pull_y = scale * along_y
-                sum_x = pull_x if sum_x is None else sum_x + pull_x
-                sum_y = pull_y if sum_y is None else sum_y + pull_y
-                if own[row_off] is None:
-                    own[row_off] = (pull_x, pull_y)
-                else:
-                    own[row_off] = (own[row_off][0] + pull_x, own[row_off][1] + pull_y)
-            push[2 * (col_off + 3), pl.ds(line, 8), :] = sum_x
-            push[2 * (col_off + 3) + 1, pl.ds(line, 8), :] = sum_y
-        for row_off in range(4):
-            pull[2 * row_off, pl.ds(line, 8), :] = own[row_off][0]
-            pull[2 * row_off + 1, pl.ds(line, 8), :] = own[row_off][1]
+                scale = mask * (STIFFNESS - (STIFFNESS * rest - dot * inverse) * inverse)
+                pulled = (scale * along_x, scale * along_y)
+                sums = [added(sums[part], pulled[part]) for part in range(2)]
+                own[row_off] = [
+                    added(own[row_off][part] if own[row_off] else None, pulled[part])
+                    for part in range(2)
+                ]
+            for part in range(2):
+                moved = sums[part]
+                if col_off:
+                    moved = pltpu.roll(moved, col_off % LANES, 1)
+                    wrapped = lanes < col_off if col_off > 0 else lanes >= LANES + col_off
+                    carry_over[part] = added(carry_over[part], jnp.where(wrapped, moved, 0.0))
+                main[part] = added(main[part], moved)
+        for part in range(2):
+            push[part, pl.ds(line, 8), :] = main[part] - carry_over[part]
+            push[2 + part, pl.ds(line, 8), :] = carry_over[part]
+            for row_off in range(4):
+                pull[2 * row_off + part, pl.ds(line, 8), :] = own[row_off][part]
         return carry
 
     lax.fori_loop(0, count, body, 0)
 
 
+def added(total, value):
+    return value if total is None else total + value
+
+
 def update_lines(data, push, pull, start, count, which, unroll):
-    lanes = lane_ids()
+    low_half = lane_ids() < LANES // 2
 
     def change(line, part):
         force = pull[part, pl.ds(line, 8), :]
         for row_off in (1, 2, 3):
             force = force + pull[2 * row_off + part, pl.ds(line + PITCH * row_off, 8), :]
-        for col_off in range(-3, 4):
-            slot = 2 * (col_off + 3) + part
-            here = push[slot, pl.ds(line, 8), :]
-            if col_off > 0:
-                here = shifted(here, None, push[slot, pl.ds(line - 1, 8), :], -col_off, lanes)
-            elif col_off < 0:
-                here = shifted(here, push[slot, pl.ds(line + 1, 8), :], None, -col_off, lanes)
-            force = force - here
-        return (0.5 * TIME_STEP) * force
+        carried = jnp.where(
+            low_half, push[2 + part, pl.ds(line - 1, 8), :], push[2 + part, pl.ds(line + 1, 8), :]
+        )
+        return (0.5 * TIME_STEP) * (force - push[part, pl.ds(line, 8), :] - carried)
 
     def body(step, carry):
         base = start + 8 * unroll * step
@@ -196,12 +202,8 @@
     lax.fori_loop(0, -(-count // unroll), body, 0)
 
 
-def step_kernel(
-    block_ref, even_ref, odd_ref, below_ref, above_ref,
-    disp_ref, vel_ref, data, masks, push, pull,
-):
-    lanes = lane_ids()
-    low_half = lanes < LANES // 2
+def first_kernel(block_ref, even_ref, odd_ref, data, masks, push, pull):
+    low_half = lane_ids() < LANES // 2
     is_even = lax.rem(lax.axis_index("gx"), 2) == 0
     even_line = jnp.where(is_even, row_line(8), row_line(-8))
     odd_line = jnp.where(is_even, row_line(-8), row_line(8))
@@ -211,25 +213,42 @@
             data[field, pl.ds(row_line(0) + 8 * part, 8), :] = block_ref[source, :]
             data[field, pl.ds(even_line + 8 * part, 8), :] = even_ref[source, :]
             data[field, pl.ds(odd_line + 8 * part, 8), :] = odd_ref[source, :]
-        ends = pl.ds(PITCH * field, PITCH)
-        data[field, pl.ds(row_line(-9), PITCH), :] = below_ref[ends, :]
-        data[field, pl.ds(row_line(16), PITCH), :] = above_ref[ends, :]
     for field in range(FIELDS):
-        lines = [
-            (row_line(-8) + 8 * PITCH * k, 8 if k < 3 else 2) for k in range(4)
-        ]
-        joined = []
-        for line, size in lines:
-            own = data[field, pl.ds(line, size, stride=PITCH), :]
-            ahead = data[field, pl.ds(line - PITCH, size, stride=PITCH), :]
-            joined.append(jnp.where(low_half[:size], ahead, own))
-        for (line, size), value in zip(lines, joined):
-            data[field, pl.ds(line, size, stride=PITCH), :] = value
+        firsts = [row_line(row) for row in (-8, 0, 8)]
+        heads = [data[field, pl.ds(line, 8, stride=PITCH), :] for line in firsts]
+        below = [data[field, pl.ds(line - PITCH, 8, stride=PITCH), :] for line in firsts]
+        final = data[field, pl.ds(row_line(15), 1), :]
+        for line, head, last in zip(firsts, heads, below):
+            data[field, pl.ds(line, 8, stride=PITCH), :] = jnp.where(low_half, last, head)
+        data[field, pl.ds(row_line(16), 1), :] = final
+    first, last = row_line(-5), row_line(16)
+    force_lines(data, masks, push, pull, first, -(-(last - first) // 8), True)
+
+
+def rest_kernel(
+    below_ref, above_ref, data_in, masks_in, push_in, pull_in,
+    disp_ref, vel_ref, data, masks, push, pull,
+):
+    low = lax.broadcasted_iota(jnp.int32, (1, LANES), 1) < LANES // 2
+    for field in range(FIELDS):
+        below = below_ref[pl.ds(PITCH * field, PITCH), :]
+        above = above_ref[pl.ds(PITCH * field, PITCH), :]
+        data[field, pl.ds(row_line(-9), PITCH), :] = below
+        head = pl.ds(row_line(-8), 1)
+        data[field, head, :] = jnp.where(low, below[:1], data[field, head, :])
+        head = pl.ds(row_line(16), 1)
+        kept = data[field, head, :]
+        data[field, pl.ds(row_line(16), PITCH), :] = above
+        data[field, head, :] = jnp.where(low, kept, above[:1])
+        data[field, pl.ds(row_line(17), 1), :] = above[:1]
+    force_lines(data, masks, push, pull, row_line(-6), 2, True)
+    force_lines(data, masks, push, pull, row_line(16), 2, True)
     for which in range(3):
         reach = 3 * (2 - which)
         low, high = -reach, ROWS + reach
         first, last = row_line(low), row_line(high + 3) + 1
-        force_lines(data, masks, push, pull, first, -(-(last - first) // 8), which == 0)
+        if which:
+            force_lines(data, masks, push, pull, first, -(-(last - first) // 8), False)
         last = row_line(high) + 1
         update_lines(data, push, pull, first, -(-(last - first) // 8), which, (4, 4, 3)[which])
     for tile in range(ROWS):
@@ -259,17 +278,17 @@
 def per_device(disp, vel, bonds):
     f32 = jnp.float32
     small = pltpu.CompilerParams(vmem_limit_bytes=4 * 2**20)
-    edge = pl.pallas_call(
+    edge, disp, vel, bonds = pl.pallas_call(
         edge_kernel,
-        out_shape=jax.ShapeDtypeStruct((8 * FIELDS, LANES), f32),
+        out_shape=(
+            jax.ShapeDtypeStruct((8 * FIELDS, LANES), f32),
+            jax.ShapeDtypeStruct(disp.shape, disp.dtype),
+            jax.ShapeDtypeStruct(vel.shape, vel.dtype),
+            jax.ShapeDtypeStruct(bonds.shape, bonds.dtype),
+        ),
         in_specs=[pl.BlockSpec(memory_space=pltpu.HBM)] * 3,
-        out_specs=VMEM,
-        scratch_shapes=[
-            pltpu.VMEM((2, 2, ROWS, LANES), f32),
-            pltpu.VMEM((2, 2, ROWS, LANES), f32),
-            pltpu.VMEM((2, 4, ROWS, LANES), jnp.int32),
-            pltpu.SemaphoreType.DMA((2, 3)),
-        ],
+        out_specs=(VMEM,) * 4,
+        scratch_shapes=[pltpu.SemaphoreType.DMA((3,))],
         compiler_params=small,
         name="edge",
     )(*(pltpu.with_memory_space_constraint(x, pltpu.HBM) for x in (disp, vel, bonds)))
@@ -288,21 +307,31 @@
     even_block = swap(block, "gx", 0)
     below = shift(last, "gx", 2)
     above = shift(first, "gx", -2)
+    work = tuple(
+        jax.ShapeDtypeStruct((count, LINES, LANES), f32) for count in (FIELDS, 24, 4, 8)
+    )
+    state = pl.pallas_call(
+        first_kernel,
+        out_shape=work,
+        in_specs=[VMEM] * 3,
+        out_specs=(VMEM,) * 4,
+        compiler_params=small,
+        cost_estimate=pl.CostEstimate(
+            flops=20_000_000, bytes_accessed=8_000_000, transcendentals=500_000
+        ),
+        name="first",
+    )(block, even_block, odd_block)
     out = jax.ShapeDtypeStruct(disp.shape, f32)
-    return pl.pallas_call(
-        step_kernel,
-        out_shape=(out, out),
-        in_specs=[VMEM] * 5,
-        out_specs=(VMEM, VMEM),
-        scratch_shapes=[
-            pltpu.VMEM((FIELDS, LINES, LANES), f32),
-            pltpu.VMEM((24, LINES, LANES), f32),
-            pltpu.VMEM((14, LINES, LANES), f32),
-            pltpu.VMEM((8, LINES, LANES), f32),
-        ],
-        compiler_params=pltpu.CompilerParams(vmem_limit_bytes=16 * 2**20),
-        name="steps",
-    )(block, even_block, odd_block, below, above)
+    results = pl.pallas_call(
+        rest_kernel,
+        out_shape=(out, out) + work,
+        in_specs=[VMEM] * 6,
+        out_specs=(VMEM,) * 6,
+        input_output_aliases={2: 2, 3: 3, 4: 4, 5: 5},
+        compiler_params=small,
+        name="rest",
+    )(below, above, *state)
+    return results[0], results[1]
 
 
 def solution(mesh):

time: 44.9 us -> 46.6 us (1.038)
  Pallas kernels: 11.5 us -> 14.7 us
  waiting for transfers between devices: 2.65 us -> 1.17 us
    pallas_call x2 -> x3, Pallas kernels: 11.5 us -> 14.7 us  [the longest x1 8.62 us: per_device(): pl.pallas_call(rest_kernel, out_shape=(out, out) + work, in_specs=[VMEM]...]
    ppermute x2, waiting for transfers between devices: 1.49 us -> 0.01 us  [shift(): lax.ppermute(array, axis, [(i, (i + by) % count) for i in range(count)])]
  transfers between devices with their start and end apart: 6 -> 6, of which waited for: 3 -> 2; matrix products, arithmetic and copies ran while one was open for 0% -> 0% of each run, Pallas kernels for 0% -> 11%
where the time goes in v3:
time: 46.6 us; the launch traced here: 46.3 us
  starting transfers between devices  29.7 us (64%)
  Pallas kernels  14.7 us (32%)
  waiting for transfers between devices  1.17 us (3%)
  between operations  0.72 us (2%)
    ppermute x4, starting transfers between devices, swap(): return lax.ppermute(array, axis, pairs)  22.6 us
    pallas_call x1, Pallas kernels, per_device(): pl.pallas_call(rest_kernel, out_shape=(out, out) + work, in_specs=[VMEM]...  8.62 us
    ppermute x2, starting transfers between devices, shift(): lax.ppermute(array, axis, [(i, (i + by) % count) for i in range(count)])  7.05 us
    pallas_call x1, Pallas kernels, per_device(): pl.pallas_call(first_kernel, out_shape=work, in_specs=[VMEM] * 3, out_spe...  5.06 us
    ppermute x4, waiting for transfers between devices, swap(): return lax.ppermute(array, axis, pairs)  1.16 us
    pallas_call x1, Pallas kernels, per_device(): pl.pallas_call(edge_kernel, out_shape=(jax.ShapeDtypeStruct((8 * FIELDS,...  1.01 us
  transfers between devices with their start and end apart: 6, of which 2 were waited for; matrix products, arithmetic and copies ran while one was open for 0% of the time, Pallas kernels for 11%

profile of v3, /device:TPU:2, one launch (start us, length us, event | category | flops | bytes accessed | tf_op | source)
XLA Modules:
  0.0 46.3 jit_solution(9668039798165641366)
XLA Ops:
  0.6 1.0 %edge.1 = (f32[40,128]{1,0:T(8,128)S(1)}, f32[2,8,1024]{2,1,0:T(8,128)S(1)}, f32[2,8,1024]{2,1,0:T(8,128)S(1)}, s32[4,8,1024]{2,1,0:T(8,128)S(1)}) custom-call(f32[2,8,1024]{2,1,0:T(8,128)} %disp_hbm.1, f32[2,8,1024]{2,1,0:T(8,128)} %vel_hbm.1, s32[4,8,1024]{2,1,0:T(8,128)} %bonds_hbm.1), custom_call_target="tpu_custom_call" | custom-call | tf_op jit(solution)/shard_map/edge/pallas_call | solution.py:281
  1.6 5.9 %collective-permute-start.1 = (f32[40,128]{1,0:T(8,128)S(1)}, f32[40,128]{1,0:T(8,128)S(1)}, u32[]{:S(2)}, u32[]{:S(2)}) collective-permute-start(f32[40,128]{1,0:T(8,128)S(1)} %get-tuple-element.18), channel_id=1, source_target_pairs={{1,2},{2,1},{3,4},{4,3},{5,6},{6,5},{7,8},{8,7},{9,10},{10,9},{11,... | collective-permute-start | bytes 61448 | tf_op jit(solution)/shard_map/ppermute | solution.py:272
  7.6 1.9 %collective-permute-start = (f32[40,128]{1,0:T(8,128)S(1)}, f32[40,128]{1,0:T(8,128)S(1)}, u32[]{:S(2)}, u32[]{:S(2)}) collective-permute-start(f32[40,128]{1,0:T(8,128)S(1)} %get-tuple-element.18), channel_id=1, source_target_pairs={{0,1},{1,0},{2,3},{3,2},{4,5},{5,4},{6,7},{7,6},{8,9},{9,8},{10,11... | collective-permute-start | bytes 61448 | tf_op jit(solution)/shard_map/ppermute | solution.py:272
  9.5 0.9 %collective-permute-done.1.odd_ref = f32[40,128]{1,0:T(8,128)S(1)} collective-permute-done((f32[40,128]{1,0:T(8,128)S(1)}, f32[40,128]{1,0:T(8,128)S(1)}, u32[]{:S(2)}, u32[]{:S(2)}) %collective-permute-start.1) | collective-permute-done | bytes 20512 | tf_op jit(solution)/shard_map/ppermute | solution.py:272
  10.4 0.3 collective-permute-done.even_ref
  10.7 4.7 %collective-permute-start.5 = (f32[360,128]{1,0:T(8,128)S(1)}, f32[360,128]{1,0:T(8,128)S(1)}, u32[]{:S(2)}, u32[]{:S(2)}) collective-permute-start(f32[360,128]{1,0:T(8,128)S(1)} %get-tuple-element.21.block_ref), channel_id=1, source_target_pairs={{16,32},{32,16},{48,64},{64,48},{80,96},{96,80},{112,128},{128,112... | collective-permute-start | bytes 552968 | tf_op jit(solution)/shard_map/ppermute | solution.py:272
  15.4 10.1 %collective-permute-start.4 = (f32[360,128]{1,0:T(8,128)S(1)}, f32[360,128]{1,0:T(8,128)S(1)}, u32[]{:S(2)}, u32[]{:S(2)}) collective-permute-start(f32[360,128]{1,0:T(8,128)S(1)} %get-tuple-element.21.block_ref), channel_id=1, source_target_pairs={{0,16},{16,0},{32,48},{48,32},{64,80},{80,64},{96,112},{112,96},{1... | collective-permute-start | bytes 552968 | tf_op jit(solution)/shard_map/ppermute | solution.py:272
  25.5 1.9 %collective-permute-start.2 = (f32[45,128]{1,0:T(8,128)S(1)}, f32[45,128]{1,0:T(8,128)S(1)}, u32[]{:S(2)}, u32[]{:S(2)}) collective-permute-start(f32[45,128]{1,0:T(8,128)S(1)} %get-tuple-element.19), channel_id=1, source_target_pairs={{0,32},{16,48},{32,64},{48,80},{64,96},{80,112},{96,128},{112,144}... | collective-permute-start | bytes 69128 | tf_op jit(solution)/shard_map/ppermute | solution.py:264
  27.4 5.1 %collective-permute-start.3 = (f32[45,128]{1,0:T(8,128)S(1)}, f32[45,128]{1,0:T(8,128)S(1)}, u32[]{:S(2)}, u32[]{:S(2)}) collective-permute-start(f32[45,128]{1,0:T(8,128)S(1)} %get-tuple-element.20), channel_id=1, source_target_pairs={{0,480},{16,496},{32,0},{48,16},{64,32},{80,48},{96,64},{112,80},{... | collective-permute-start | bytes 69128 | tf_op jit(solution)/shard_map/ppermute | solution.py:264
  32.6 0.0 collective-permute-done.5.odd_ref
  32.6 0.0 collective-permute-done.4.even_ref
  32.6 5.1 %first.1 = (f32[5,256,128]{2,1,0:T(8,128)S(1)}, f32[24,256,128]{2,1,0:T(8,128)S(1)}, f32[4,256,128]{2,1,0:T(8,128)S(1)}, f32[8,256,128]{2,1,0:T(8,128)S(1)}) custom-call(f32[360,128]{1,0:T(8,128)S(1)} %get-tuple-element.21.block_ref, f32[360,128]{1,0:T(8,128)S(1)} %collective-permute-done.4.even_ref, f32[360,128]{1,0:T(8,128)S(1)} %collective-permute-done.5.odd_ref), custom_call_target="tpu_custom_call" | custom-call | flops 20000000 | bytes 8000000 | tf_op jit(solution)/shard_map/first/pallas_call | solution.py:313
  37.6 0.0 collective-permute-done.2.below_ref
  37.7 0.0 collective-permute-done.3.above_ref
  37.7 8.6 %rest.1 = (f32[2,8,1024]{2,1,0:T(8,128)}, f32[2,8,1024]{2,1,0:T(8,128)}, f32[5,256,128]{2,1,0:T(8,128)S(1)}, f32[24,256,128]{2,1,0:T(8,128)S(1)}, f32[4,256,128]...) custom-call(f32[45,128]{1,0:T(8,128)S(1)} %collective-permute-done.2, ...), custom_call_target="tpu_custom_call", output_to_operand_aliasing={{2}: (2, {}), {3}: (3, {}), {4}: (4, {}), {5}: (5, {})} | custom-call | tf_op jit(solution)/shard_map/rest/pallas_call | solution.py:325
  (1 shorter events, 0.0 us)
Async XLA Ops:
  1.6 8.7 %collective-permute-start.1 = (f32[40,128]{1,0:T(8,128)S(1)}, f32[40,128]{1,0:T(8,128)S(1)}, u32[]{:S(2)}, u32[]{:S(2)}) collective-permute-start(f32[40,128]{1,0:T(8,128)S(1)} %get-tuple-element.18), channel_id=1, source_target_pairs={{1,2},{2,1},{3,4},{4,3},{5,6},{6,5},{7,8},{8,7},{9,10},{10,9},{11,... | collective-permute-start | bytes 61448 | tf_op jit(solution)/shard_map/ppermute | solution.py:272
  7.6 3.1 %collective-permute-start = (f32[40,128]{1,0:T(8,128)S(1)}, f32[40,128]{1,0:T(8,128)S(1)}, u32[]{:S(2)}, u32[]{:S(2)}) collective-permute-start(f32[40,128]{1,0:T(8,128)S(1)} %get-tuple-element.18), channel_id=1, source_target_pairs={{0,1},{1,0},{2,3},{3,2},{4,5},{5,4},{6,7},{7,6},{8,9},{9,8},{10,11... | collective-permute-start | bytes 61448 | tf_op jit(solution)/shard_map/ppermute | solution.py:272
  10.7 21.9 %collective-permute-start.5 = (f32[360,128]{1,0:T(8,128)S(1)}, f32[360,128]{1,0:T(8,128)S(1)}, u32[]{:S(2)}, u32[]{:S(2)}) collective-permute-start(f32[360,128]{1,0:T(8,128)S(1)} %get-tuple-element.21.block_ref), channel_id=1, source_target_pairs={{16,32},{32,16},{48,64},{64,48},{80,96},{96,80},{112,128},{128,112... | collective-permute-start | bytes 552968 | tf_op jit(solution)/shard_map/ppermute | solution.py:272
  15.4 17.2 %collective-permute-start.4 = (f32[360,128]{1,0:T(8,128)S(1)}, f32[360,128]{1,0:T(8,128)S(1)}, u32[]{:S(2)}, u32[]{:S(2)}) collective-permute-start(f32[360,128]{1,0:T(8,128)S(1)} %get-tuple-element.21.block_ref), channel_id=1, source_target_pairs={{0,16},{16,0},{32,48},{48,32},{64,80},{80,64},{96,112},{112,96},{1... | collective-permute-start | bytes 552968 | tf_op jit(solution)/shard_map/ppermute | solution.py:272
  25.5 12.2 %collective-permute-start.2 = (f32[45,128]{1,0:T(8,128)S(1)}, f32[45,128]{1,0:T(8,128)S(1)}, u32[]{:S(2)}, u32[]{:S(2)}) collective-permute-start(f32[45,128]{1,0:T(8,128)S(1)} %get-tuple-element.19), channel_id=1, source_target_pairs={{0,32},{16,48},{32,64},{48,80},{64,96},{80,112},{96,128},{112,144}... | collective-permute-start | bytes 69128 | tf_op jit(solution)/shard_map/ppermute | solution.py:264
  27.4 10.2 %collective-permute-start.3 = (f32[45,128]{1,0:T(8,128)S(1)}, f32[45,128]{1,0:T(8,128)S(1)}, u32[]{:S(2)}, u32[]{:S(2)}) collective-permute-start(f32[45,128]{1,0:T(8,128)S(1)} %get-tuple-element.20), channel_id=1, source_target_pairs={{0,480},{16,496},{32,0},{48,16},{64,32},{80,48},{96,64},{112,80},{... | collective-permute-start | bytes 69128 | tf_op jit(solution)/shard_map/ppermute | solution.py:264

commit v4 on v3

v4 whole, which is shorter than its diff:
```python
import math

import jax
import jax.numpy as jnp
from jax import lax
from jax.experimental import pallas as pl
from jax.experimental.pallas import tpu as pltpu
from jax.sharding import PartitionSpec as P

STIFFNESS = 40.0
TIME_STEP = 0.05
SOFTENING = 0.0625
PACK_SHIFT = (0, 3, 10, 17)
LANES = 128

ROWS = 8
PITCH = 9
BLOCK = ROWS * PITCH
FIELDS = 5
HALO = 9
GUARD = 8
LINES = 256


def row_line(row):
    return GUARD + PITCH * (row + HALO)


def lane_ids():
    return lax.broadcasted_iota(jnp.int32, (8, LANES), 1)


def edge_kernel(disp_hbm, vel_hbm, bonds_hbm, edge_ref, disp, vel, bonds, sems):
    copies = [
        pltpu.make_async_copy(source, target, sems.at[k])
        for k, (source, target) in enumerate(
            ((disp_hbm, disp), (vel_hbm, vel), (bonds_hbm, bonds))
        )
    ]
    for copy in copies:
        copy.start()
    for copy in copies:
        copy.wait()
    low_half = lane_ids() < LANES // 2
    left = pl.ds(0, LANES)
    right = pl.ds((ROWS - 1) * LANES, LANES)

    def ends(ref, part):
        return jnp.where(low_half, ref[part, :, left], ref[part, :, right])

    for part in range(2):
        edge_ref[pl.ds(8 * part, 8), :] = ends(disp, part)
        edge_ref[pl.ds(8 * part + 16, 8), :] = ends(vel, part)
    edge_ref[pl.ds(32, 8), :] = packed([ends(bonds, word) for word in range(4)])


def packed(words):
    total = words[0]
    for word in (1, 2, 3):
        total = total + words[word] * (1 << PACK_SHIFT[word])
    return total.astype(jnp.float32)


def block_kernel(disp_ref, vel_ref, bonds_ref, even_ref, odd_ref, block_ref, first_ref, last_ref):
    low_half = lane_ids() < LANES // 2
    is_even = lax.rem(lax.axis_index("gy"), 2) == 0
    for field in range(FIELDS):
        even = even_ref[pl.ds(8 * field, 8), :]
        odd = odd_ref[pl.ds(8 * field, 8), :]
        from_right = jnp.where(is_even, even, odd)
        from_left = jnp.where(is_even, odd, even)
        lines = [jnp.where(low_half, from_right, from_left)]
        for tile in range(ROWS):
            cols = pl.ds(tile * LANES, LANES)
            if field < 2:
                lines.append(disp_ref[field, :, cols])
            elif field < 4:
                lines.append(vel_ref[field - 2, :, cols])
            else:
                lines.append(packed([bonds_ref[word, :, cols] for word in range(4)]))
        for k, value in enumerate(lines):
            block_ref[pl.ds(field * BLOCK + k, ROWS, stride=PITCH), :] = value
            first_ref[pl.ds(PITCH * field + k, 1), :] = value[:1]
            last_ref[pl.ds(PITCH * field + k, 1), :] = value[7:]


def look_ahead(data, words, ahead, ahead_words, line, lanes, with_words):
    found = []
    here = [data[f, pl.ds(line, 8), :] for f in range(4)]
    after = [data[f, pl.ds(line + 1, 8), :] for f in range(4)]
    for by in (1, 2, 3):
        far = []
        for f in range(4):
            value = pltpu.roll(jnp.where(lanes < by, after[f], here[f]), LANES - by, 1)
            if f == 1:
                value = value + float(by)
            ahead[4 * (by - 1) + f, pl.ds(line, 8), :] = value
            far.append(value)
        found.append(far)
        if with_words:
            ahead_words[by - 1, pl.ds(line, 8), :] = pltpu.roll(
                jnp.where(lanes < by, words[pl.ds(line + 1, 8), :], words[pl.ds(line, 8), :]),
                LANES - by,
                1,
            )
    return here, found


def prepare_lines(data, words, ahead, ahead_words, start, count, with_words):
    lanes = lane_ids()
    for step in range(count):
        look_ahead(data, words, ahead, ahead_words, start + 8 * step, lanes, with_words)


def bond_pull(far, near, row_off, col_off, mask):
    rest = math.sqrt(row_off * row_off + col_off * col_off + SOFTENING)
    along_x = far[0] - near[0]
    along_y = far[1] - near[1]
    rate_x = far[2] - near[2]
    rate_y = far[3] - near[3]
    inverse = lax.rsqrt(along_x * along_x + (along_y * along_y + SOFTENING))
    dot = along_x * rate_x + along_y * rate_y
    scale = mask * (STIFFNESS - (STIFFNESS * rest - dot * inverse) * inverse)
    return (scale * along_x, scale * along_y)


def added(total, value):
    if total is None:
        return list(value)
    return [total[part] + value[part] for part in range(2)]


def force_lines(state, start, count, fresh_masks):
    data, words, ahead, ahead_words, masks, pull, push = state
    lanes = lane_ids()

    def body(step, carry):
        line = start + 8 * step
        here, found = look_ahead(data, words, ahead, ahead_words, line, lanes, fresh_masks)

        def at(ref, k, offset):
            return ref[k, pl.ds(line - PITCH * offset, 8), :]

        def mask_of(slot, row_off, col_off, word):
            if not fresh_masks:
                return masks[slot, pl.ds(line, 8), :]
            weight = 1.0 / (row_off * row_off + col_off * col_off)
            mask = jnp.where((word & (1 << slot)) != 0, weight, 0.0)
            masks[slot, pl.ds(line, 8), :] = mask
            return mask

        def store(ref, k, value):
            for part in range(2):
                ref[2 * k + part, pl.ds(line, 8), :] = value[part]

        own = [None] * 4
        reach = [None] * 4
        for row_off in range(4):
            near = here if row_off == 0 else [at(data, f, row_off) for f in range(4)]
            if row_off:
                near[0] = near[0] - float(row_off)
            word = words[pl.ds(line - PITCH * row_off, 8), :] if fresh_masks else None
            for col_off in range(4):
                if row_off == 0 and col_off == 0:
                    continue
                far = found[col_off - 1] if col_off else here
                slot = col_off - 1 if row_off == 0 else PACK_SHIFT[row_off] + col_off + 3
                mask = mask_of(slot, row_off, col_off, word)
                value = bond_pull(far, near, row_off, col_off, mask)
                own[row_off] = added(own[row_off], value)
                reach[col_off] = added(reach[col_off], value)
        for col_off in range(4):
            store(push, col_off, reach[col_off])
        for row_off in (1, 2, 3):
            near = [here[0] + float(row_off)] + list(here[1:])
            for col_off in (1, 2, 3):
                far = [at(ahead, 4 * (col_off - 1) + f, row_off) for f in range(4)]
                slot = PACK_SHIFT[row_off] - col_off + 3
                word = at(ahead_words, col_off - 1, row_off) if fresh_masks else None
                mask = mask_of(slot, row_off, col_off, word)
                value = bond_pull(far, near, row_off, col_off, mask)
                own[0] = added(own[0], value)
                store(push, 3 * row_off + col_off, value)
        for row_off in range(4):
            store(pull, row_off, own[row_off])
        return carry

    lax.fori_loop(0, count, body, 0)


def update_lines(state, over, start, count, which, unroll):
    data, _, _, _, _, pull, push = state
    lanes = lane_ids()

    def force_at(line, part):
        def at(ref, k, offset):
            return ref[2 * k + part, pl.ds(line + PITCH * offset, 8), :]

        force = at(pull, 0, 0) - at(push, 0, 0)
        for row_off in (1, 2, 3):
            force = force + at(pull, row_off, row_off)
        wrapped = None
        for col_off in (1, 2, 3):
            total = at(push, col_off, 0)
            for row_off in (1, 2, 3):
                total = total + at(push, 3 * row_off + col_off, row_off)
            total = pltpu.roll(total, col_off, 1)
            inside = lanes >= col_off
            force = force - jnp.where(inside, total, 0.0)
            outside = jnp.where(inside, 0.0, total)
            wrapped = outside if wrapped is None else wrapped + outside
        over[part, pl.ds(line, 8), :] = wrapped
        return force

    def body(step, carry):
        base = start + 8 * unroll * step
        lines = [base + 8 * k for k in range(unroll)]
        forces = [[force_at(line, part) for part in range(2)] for line in lines]
        stores = []
        for line, both in zip(lines, forces):
            for part in range(2):
                gain = (0.5 * TIME_STEP) * (both[part] - over[part, pl.ds(line - 1, 8), :])
                speed = data[2 + part, pl.ds(line, 8), :] + gain
                if which == 1:
                    speed = speed + gain
                stores.append((2 + part, line, speed))
                if which < 2:
                    moved = data[part, pl.ds(line, 8), :] + TIME_STEP * speed
                    stores.append((part, line, moved))
        for field, line, value in stores:
            data[field, pl.ds(line, 8), :] = value
        return carry

    lax.fori_loop(0, -(-count // unroll), body, 0)


def first_kernel(block_ref, even_ref, odd_ref, *state):
    data, words = state[:2]
    low_half = lane_ids() < LANES // 2
    is_even = lax.rem(lax.axis_index("gx"), 2) == 0
    even_line = jnp.where(is_even, row_line(8), row_line(-8))
    odd_line = jnp.where(is_even, row_line(-8), row_line(8))

    def get(field, lines):
        return data[field, lines, :] if field < 4 else words[lines, :]

    def put(field, lines, value):
        if field < 4:
            data[field, lines, :] = value
        else:
            words[lines, :] = value

    for field in range(FIELDS):
        for part in range(PITCH):
            source = pl.ds(field * BLOCK + 8 * part, 8)
            for ref, line in (
                (block_ref, row_line(0)), (even_ref, even_line), (odd_ref, odd_line)
            ):
                value = ref[source, :]
                if field == 4:
                    value = value.astype(jnp.int32)
                put(field, pl.ds(line + 8 * part, 8), value)
    for field in range(FIELDS):
        firsts = [row_line(row) for row in (-8, 0, 8)]
        heads = [get(field, pl.ds(line, 8, stride=PITCH)) for line in firsts]
        below = [get(field, pl.ds(line - PITCH, 8, stride=PITCH)) for line in firsts]
        final = get(field, pl.ds(row_line(15), 1))
        for line, head, last in zip(firsts, heads, below):
            put(field, pl.ds(line, 8, stride=PITCH), jnp.where(low_half, last, head))
        put(field, pl.ds(row_line(16), 1), final)
    first, last = row_line(-5), row_line(16)
    prepare_lines(*state[:4], row_line(-8), 4, True)
    force_lines(state, first, -(-(last - first) // 8), True)


def rest_kernel(below_ref, above_ref, *refs):
    count = len(refs) - 3
    state_count = count // 2
    disp_ref, vel_ref = refs[state_count : state_count + 2]
    state = refs[state_count + 2 : -1]
    over = refs[-1]
    data, words = state[:2]
    low = lax.broadcasted_iota(jnp.int32, (1, LANES), 1) < LANES // 2
    for field in range(FIELDS):
        below = below_ref[pl.ds(PITCH * field, PITCH), :]
        above = above_ref[pl.ds(PITCH * field, PITCH), :]
        if field == 4:
            below, above = below.astype(jnp.int32), above.astype(jnp.int32)
        target = data.at[field] if field < 4 else words
        target[pl.ds(row_line(-9), PITCH), :] = below
        head = pl.ds(row_line(-8), 1)
        target[head, :] = jnp.where(low, below[:1], target[head, :])
        head = pl.ds(row_line(16), 1)
        kept = target[head, :]
        target[pl.ds(row_line(16), PITCH), :] = above
        target[head, :] = jnp.where(low, kept, above[:1])
        target[pl.ds(row_line(17), 1), :] = above[:1]
    prepare_lines(*state[:4], row_line(-9), 4, True)
    force_lines(state, row_line(-6), 2, True)
    force_lines(state, row_line(16), 2, True)
    for which in range(3):
        reach = 3 * (2 - which)
        low_row, high_row = -reach, ROWS + reach
        first, last = row_line(low_row), row_line(high_row + 3) + 1
        if which:
            prepare_lines(*state[:4], row_line(low_row - 3), 4, False)
            force_lines(state, first, -(-(last - first) // 8), False)
        last = row_line(high_row) + 1
        update_lines(state, over, first, -(-(last - first) // 8), which, (4, 4, 3)[which])
    for tile in range(ROWS):
        lines = pl.ds(row_line(0) + 1 + tile, ROWS, stride=PITCH)
        cols = pl.ds(tile * LANES, LANES)
        for part in range(2):
            disp_ref[part, :, cols] = data[part, lines, :]
            vel_ref[part, :, cols] = data[2 + part, lines, :]


def shift(array, axis, by):
    count = lax.axis_size(axis)
    return lax.ppermute(array, axis, [(i, (i + by) % count) for i in range(count)])


def swap(array, axis, odd):
    count = lax.axis_size(axis)
    pairs = []
    for i in range(odd, count + odd, 2):
        pairs += [(i % count, (i + 1) % count), ((i + 1) % count, i % count)]
    return lax.ppermute(array, axis, pairs)


VMEM = pl.BlockSpec(memory_space=pltpu.VMEM)


def per_device(disp, vel, bonds):
    f32 = jnp.float32
    small = pltpu.CompilerParams(vmem_limit_bytes=4 * 2**20)
    edge, disp, vel, bonds = pl.pallas_call(
        edge_kernel,
        out_shape=(
            jax.ShapeDtypeStruct((8 * FIELDS, LANES), f32),
            jax.ShapeDtypeStruct(disp.shape, disp.dtype),
            jax.ShapeDtypeStruct(vel.shape, vel.dtype),
            jax.ShapeDtypeStruct(bonds.shape, bonds.dtype),
        ),
        in_specs=[pl.BlockSpec(memory_space=pltpu.HBM)] * 3,
        out_specs=(VMEM,) * 4,
        scratch_shapes=[pltpu.SemaphoreType.DMA((3,))],
        compiler_params=small,
        name="edge",
    )(*(pltpu.with_memory_space_constraint(x, pltpu.HBM) for x in (disp, vel, bonds)))
    odd_edge = swap(edge, "gy", 1)
    even_edge = swap(edge, "gy", 0)
    ends = jax.ShapeDtypeStruct((FIELDS * PITCH, LANES), f32)
    block, first, last = pl.pallas_call(
        block_kernel,
        out_shape=(jax.ShapeDtypeStruct((FIELDS * BLOCK, LANES), f32), ends, ends),
        in_specs=[VMEM] * 5,
        out_specs=(VMEM,) * 3,
        compiler_params=small,
        name="block",
    )(disp, vel, bonds, even_edge, odd_edge)
    odd_block = swap(block, "gx", 1)
    even_block = swap(block, "gx", 0)
    below = shift(last, "gx", 2)
    above = shift(first, "gx", -2)
    work = (
        jax.ShapeDtypeStruct((4, LINES, LANES), f32),
        jax.ShapeDtypeStruct((LINES, LANES), jnp.int32),
        jax.ShapeDtypeStruct((12, LINES, LANES), f32),
        jax.ShapeDtypeStruct((3, LINES, LANES), jnp.int32),
        jax.ShapeDtypeStruct((24, LINES, LANES), f32),
        jax.ShapeDtypeStruct((8, LINES, LANES), f32),
        jax.ShapeDtypeStruct((26, LINES, LANES), f32),
    )
    state = pl.pallas_call(
        first_kernel,
        out_shape=work,
        in_specs=[VMEM] * 3,
        out_specs=(VMEM,) * len(work),
        compiler_params=small,
        cost_estimate=pl.CostEstimate(
            flops=20_000_000, bytes_accessed=8_000_000, transcendentals=500_000
        ),
        name="first",
    )(block, even_block, odd_block)
    out = jax.ShapeDtypeStruct(disp.shape, f32)
    results = pl.pallas_call(
        rest_kernel,
        out_shape=(out, out) + work,
        in_specs=[VMEM] * (2 + len(work)),
        out_specs=(VMEM,) * (2 + len(work)),
        scratch_shapes=[pltpu.VMEM((2, LINES, LANES), f32)],
        input_output_aliases={2 + k: 2 + k for k in range(len(work))},
        compiler_params=small,
        name="rest",
    )(below, above, *state)
    return results[0], results[1]


def solution(mesh):
    spec = P(None, "gx", "gy")
    return jax.shard_map(
        per_device,
        mesh=mesh,
        in_specs=(spec, spec, spec),
        out_specs=(spec, spec),
        check_vma=False,
    )
```

time: 46.6 us -> 43 us (0.923)
  Pallas kernels: 14.7 us -> 11.2 us
    pallas_call x1, Pallas kernels: 5.06 us -> 3.01 us  [per_device(): pl.pallas_call(first_kernel, out_shape=work, in_specs=[VMEM] * 3, out_spe...]
    pallas_call x1, Pallas kernels: 8.62 us -> 7.11 us  [per_device(): pl.pallas_call(rest_kernel, out_shape=(out, out) + work, in_specs=[VMEM]...]
  transfers between devices with their start and end apart: 6 -> 6, of which waited for: 2 -> 2; matrix products, arithmetic and copies ran while one was open for 0% -> 0% of each run, Pallas kernels for 11% -> 7%
where the time goes in v4:
time: 43 us; the launch traced here: 42.7 us
  starting transfers between devices  29.7 us (69%)
  Pallas kernels  11.2 us (26%)
  waiting for transfers between devices  1.17 us (3%)
  between operations  0.73 us (2%)
    ppermute x4, starting transfers between devices, swap(): return lax.ppermute(array, axis, pairs)  22.6 us
    pallas_call x1, Pallas kernels, per_device(): pl.pallas_call(rest_kernel, out_shape=(out, out) + work, in_specs=[VMEM]...  7.11 us
    ppermute x2, starting transfers between devices, shift(): lax.ppermute(array, axis, [(i, (i + by) % count) for i in range(count)])  7.05 us
    pallas_call x1, Pallas kernels, per_device(): pl.pallas_call(first_kernel, out_shape=work, in_specs=[VMEM] * 3, out_spe...  3.01 us
    ppermute x4, waiting for transfers between devices, swap(): return lax.ppermute(array, axis, pairs)  1.16 us
    pallas_call x1, Pallas kernels, per_device(): pl.pallas_call(edge_kernel, out_shape=(jax.ShapeDtypeStruct((8 * FIELDS,...  1.01 us
  transfers between devices with their start and end apart: 6, of which 2 were waited for; matrix products, arithmetic and copies ran while one was open for 0% of the time, Pallas kernels for 7%

profile of v4, /device:TPU:2, one launch (start us, length us, event | category | flops | bytes accessed | tf_op | source)
XLA Modules:
  0.0 42.7 jit_solution(14321081993366329545)
XLA Ops:
  0.6 1.0 %edge.1 = (f32[40,128]{1,0:T(8,128)S(1)}, f32[2,8,1024]{2,1,0:T(8,128)S(1)}, f32[2,8,1024]{2,1,0:T(8,128)S(1)}, s32[4,8,1024]{2,1,0:T(8,128)S(1)}) custom-call(f32[2,8,1024]{2,1,0:T(8,128)} %disp_hbm.1, f32[2,8,1024]{2,1,0:T(8,128)} %vel_hbm.1, s32[4,8,1024]{2,1,0:T(8,128)} %bonds_hbm.1), custom_call_target="tpu_custom_call" | custom-call | tf_op jit(solution)/shard_map/edge/pallas_call | solution.py:337
  1.6 5.9 %collective-permute-start.1 = (f32[40,128]{1,0:T(8,128)S(1)}, f32[40,128]{1,0:T(8,128)S(1)}, u32[]{:S(2)}, u32[]{:S(2)}) collective-permute-start(f32[40,128]{1,0:T(8,128)S(1)} %get-tuple-element.21), channel_id=1, source_target_pairs={{1,2},{2,1},{3,4},{4,3},{5,6},{6,5},{7,8},{8,7},{9,10},{10,9},{11,... | collective-permute-start | bytes 61448 | tf_op jit(solution)/shard_map/ppermute | solution.py:328
  7.6 1.9 %collective-permute-start = (f32[40,128]{1,0:T(8,128)S(1)}, f32[40,128]{1,0:T(8,128)S(1)}, u32[]{:S(2)}, u32[]{:S(2)}) collective-permute-start(f32[40,128]{1,0:T(8,128)S(1)} %get-tuple-element.21), channel_id=1, source_target_pairs={{0,1},{1,0},{2,3},{3,2},{4,5},{5,4},{6,7},{7,6},{8,9},{9,8},{10,11... | collective-permute-start | bytes 61448 | tf_op jit(solution)/shard_map/ppermute | solution.py:328
  9.5 0.9 %collective-permute-done.1.odd_ref = f32[40,128]{1,0:T(8,128)S(1)} collective-permute-done((f32[40,128]{1,0:T(8,128)S(1)}, f32[40,128]{1,0:T(8,128)S(1)}, u32[]{:S(2)}, u32[]{:S(2)}) %collective-permute-start.1) | collective-permute-done | bytes 20512 | tf_op jit(solution)/shard_map/ppermute | solution.py:328
  10.4 0.3 collective-permute-done.even_ref
  10.7 4.7 %collective-permute-start.5 = (f32[360,128]{1,0:T(8,128)S(1)}, f32[360,128]{1,0:T(8,128)S(1)}, u32[]{:S(2)}, u32[]{:S(2)}) collective-permute-start(f32[360,128]{1,0:T(8,128)S(1)} %get-tuple-element.24.block_ref), channel_id=1, source_target_pairs={{16,32},{32,16},{48,64},{64,48},{80,96},{96,80},{112,128},{128,112... | collective-permute-start | bytes 552968 | tf_op jit(solution)/shard_map/ppermute | solution.py:328
  15.4 10.1 %collective-permute-start.4 = (f32[360,128]{1,0:T(8,128)S(1)}, f32[360,128]{1,0:T(8,128)S(1)}, u32[]{:S(2)}, u32[]{:S(2)}) collective-permute-start(f32[360,128]{1,0:T(8,128)S(1)} %get-tuple-element.24.block_ref), channel_id=1, source_target_pairs={{0,16},{16,0},{32,48},{48,32},{64,80},{80,64},{96,112},{112,96},{1... | collective-permute-start | bytes 552968 | tf_op jit(solution)/shard_map/ppermute | solution.py:328
  25.5 1.9 %collective-permute-start.2 = (f32[45,128]{1,0:T(8,128)S(1)}, f32[45,128]{1,0:T(8,128)S(1)}, u32[]{:S(2)}, u32[]{:S(2)}) collective-permute-start(f32[45,128]{1,0:T(8,128)S(1)} %get-tuple-element.22), channel_id=1, source_target_pairs={{0,32},{16,48},{32,64},{48,80},{64,96},{80,112},{96,128},{112,144}... | collective-permute-start | bytes 69128 | tf_op jit(solution)/shard_map/ppermute | solution.py:320
  27.4 5.1 %collective-permute-start.3 = (f32[45,128]{1,0:T(8,128)S(1)}, f32[45,128]{1,0:T(8,128)S(1)}, u32[]{:S(2)}, u32[]{:S(2)}) collective-permute-start(f32[45,128]{1,0:T(8,128)S(1)} %get-tuple-element.23), channel_id=1, source_target_pairs={{0,480},{16,496},{32,0},{48,16},{64,32},{80,48},{96,64},{112,80},{... | collective-permute-start | bytes 69128 | tf_op jit(solution)/shard_map/ppermute | solution.py:320
  32.6 0.0 collective-permute-done.5.odd_ref
  32.6 0.0 collective-permute-done.4.even_ref
  32.6 3.0 %first.1 = (f32[4,256,128]{2,1,0:T(8,128)S(1)}, s32[256,128]{1,0:T(8,128)S(1)}, f32[12,256,128]{2,1,0:T(8,128)S(1)}, s32[3,256,128]{2,1,0:T(8,128)S(1)}, f32[24,...) custom-call(f32[360,128]{1,0:T(8,128)S(1)} %get-tuple-element.24.block_ref, ...), custom_call_target="tpu_custom_call" | custom-call | flops 20000000 | bytes 8000000 | tf_op jit(solution)/shard_map/first/pallas_call | solution.py:375
  35.6 0.0 collective-permute-done.2.below_ref
  35.6 0.0 collective-permute-done.3.above_ref
  35.6 7.1 %rest.1 = (f32[2,8,1024]{2,1,0:T(8,128)}, f32[2,8,1024]{2,1,0:T(8,128)}, f32[4,256,128]{2,1,0:T(8,128)S(1)}, s32[256,128]{1,0:T(8,128)S(1)}, f32[12,256,128]{2,1...) custom-call(f32[45,128]{1,0:T(8,128)S(1)} %collective-permute-done.2, ...), custom_call_target="tpu_custom_call", output_to_operand_aliasing={{2}: (2, {}), {3}: (3, {}), {4}: (4, {}), {5}: (5, {}), {6}... | custom-call | tf_op jit(solution)/shard_map/rest/pallas_call | solution.py:387
  (1 shorter events, 0.0 us)
Async XLA Ops:
  1.6 8.7 %collective-permute-start.1 = (f32[40,128]{1,0:T(8,128)S(1)}, f32[40,128]{1,0:T(8,128)S(1)}, u32[]{:S(2)}, u32[]{:S(2)}) collective-permute-start(f32[40,128]{1,0:T(8,128)S(1)} %get-tuple-element.21), channel_id=1, source_target_pairs={{1,2},{2,1},{3,4},{4,3},{5,6},{6,5},{7,8},{8,7},{9,10},{10,9},{11,... | collective-permute-start | bytes 61448 | tf_op jit(solution)/shard_map/ppermute | solution.py:328
  7.6 3.1 %collective-permute-start = (f32[40,128]{1,0:T(8,128)S(1)}, f32[40,128]{1,0:T(8,128)S(1)}, u32[]{:S(2)}, u32[]{:S(2)}) collective-permute-start(f32[40,128]{1,0:T(8,128)S(1)} %get-tuple-element.21), channel_id=1, source_target_pairs={{0,1},{1,0},{2,3},{3,2},{4,5},{5,4},{6,7},{7,6},{8,9},{9,8},{10,11... | collective-permute-start | bytes 61448 | tf_op jit(solution)/shard_map/ppermute | solution.py:328
  10.7 21.9 %collective-permute-start.5 = (f32[360,128]{1,0:T(8,128)S(1)}, f32[360,128]{1,0:T(8,128)S(1)}, u32[]{:S(2)}, u32[]{:S(2)}) collective-permute-start(f32[360,128]{1,0:T(8,128)S(1)} %get-tuple-element.24.block_ref), channel_id=1, source_target_pairs={{16,32},{32,16},{48,64},{64,48},{80,96},{96,80},{112,128},{128,112... | collective-permute-start | bytes 552968 | tf_op jit(solution)/shard_map/ppermute | solution.py:328
  15.4 17.2 %collective-permute-start.4 = (f32[360,128]{1,0:T(8,128)S(1)}, f32[360,128]{1,0:T(8,128)S(1)}, u32[]{:S(2)}, u32[]{:S(2)}) collective-permute-start(f32[360,128]{1,0:T(8,128)S(1)} %get-tuple-element.24.block_ref), channel_id=1, source_target_pairs={{0,16},{16,0},{32,48},{48,32},{64,80},{80,64},{96,112},{112,96},{1... | collective-permute-start | bytes 552968 | tf_op jit(solution)/shard_map/ppermute | solution.py:328
  25.5 10.1 %collective-permute-start.2 = (f32[45,128]{1,0:T(8,128)S(1)}, f32[45,128]{1,0:T(8,128)S(1)}, u32[]{:S(2)}, u32[]{:S(2)}) collective-permute-start(f32[45,128]{1,0:T(8,128)S(1)} %get-tuple-element.22), channel_id=1, source_target_pairs={{0,32},{16,48},{32,64},{48,80},{64,96},{80,112},{96,128},{112,144}... | collective-permute-start | bytes 69128 | tf_op jit(solution)/shard_map/ppermute | solution.py:320
  27.4 8.2 %collective-permute-start.3 = (f32[45,128]{1,0:T(8,128)S(1)}, f32[45,128]{1,0:T(8,128)S(1)}, u32[]{:S(2)}, u32[]{:S(2)}) collective-permute-start(f32[45,128]{1,0:T(8,128)S(1)} %get-tuple-element.23), channel_id=1, source_target_pairs={{0,480},{16,496},{32,0},{48,16},{64,32},{80,48},{96,64},{112,80},{... | collective-permute-start | bytes 69128 | tf_op jit(solution)/shard_map/ppermute | solution.py:320
